TPU v7x, 1024 devices: a whole 8x8x8 slice. The times are simulated.
1024 devices in a mesh: replica: 64 (over z, y_lo, core), fsdp: 16 (over x, y_hi).
Axes of the slice: x: 8, y: 8 (y_hi: 2, y_lo: 4; y = y_hi * 4 + y_lo), z: 8, core: 2. Of those that a mesh axis runs over, the one named last changes fastest.
Arguments:
- tokens: bfloat16 [131072, 8192], P(('replica', 'fsdp')), may hold values from -6 to 6
- norm_gain: bfloat16 [8192], P('fsdp'), may hold values from 0.099609375 to 1.8984375
- key_weight: bfloat16 [8192, 128], P('fsdp'), may hold values from -0.0625 to 0.0625
- key_cotangent: bfloat16 [131072, 128], P(('replica', 'fsdp')), may hold values from -0.25 to 0.25
- outer_params: float32 [32, 16, 8192], P(None, 'fsdp'), may hold values from -6 to 6
- outer_momentum: float32 [32, 16, 8192], P(None, 'fsdp'), may hold values from -3 to 3
- inner_params: bfloat16 [64, 32, 16, 8192], P('replica', None, 'fsdp'), may hold values from -16 to 16
- fragment: int32 [], replicated, may hold values from 0 to 31
- mix_step: int32 [64], P('replica'), may hold values from 0 to 8
Outputs:
- keys: bfloat16 [131072, 128], P(('replica', 'fsdp'))
- weight_grad: float32 [64, 8192, 128], P('replica', 'fsdp')
- gain_grad: float32 [64, 8192], P('replica', 'fsdp')
- new_outer: float32 [16, 8192], P('fsdp', 'replica')
- new_momentum: float32 [16, 8192], P('fsdp', 'replica')
- new_inner: bfloat16 [64, 16, 8192], P('replica', 'fsdp')
All inputs are finite; a program needn't handle non-finite values.
Results may differ from a plain program's by a relative error of at most 0.012.
Values may be sent and summed in bfloat16 or wider, within the bound.
No kernel may reach another device: no remote copies, remote signals or barrier semaphores. Data moves between devices by JAX's collectives and lax.ppermute only.
A program may use at most 32 MiB of HBM per device.

v0:
```python
import jax
import jax.numpy as jnp
from jax import lax
from jax.sharding import PartitionSpec as P

MIXSTEPS = 8


norm_eps = 1e-05


def on_device(
    tokens,
    norm_gain,
    key_weight,
    key_cotangent,
    outer_params,
    outer_momentum,
    inner_params,
    fragment,
    mix_step,
):
    tok_float = tokens.astype(jnp.float32)
    inv_rms = lax.rsqrt(jnp.mean(tok_float * tok_float, axis=1, keepdims=True) + norm_eps)
    unit_rows = (tok_float * inv_rms).astype(jnp.bfloat16)
    full_weight, full_gain = (
        lax.all_gather(key_weight, "fsdp", axis=0, tiled=True),
        lax.all_gather(norm_gain, "fsdp", axis=0, tiled=True),
    )
    normed = (unit_rows.astype(jnp.float32) * full_gain.astype(jnp.float32)).astype(jnp.bfloat16)
    key_out = jnp.dot(normed, full_weight, preferred_element_type=jnp.float32).astype(jnp.bfloat16)
    weight_part = lax.dot_general(
        normed, key_cotangent, (((0,), (0,)), ((), ())), preferred_element_type=jnp.float32
    )
    grad_normed = lax.dot_general(
        key_cotangent, full_weight, (((1,), (1,)), ((), ())), preferred_element_type=jnp.float32
    )
    gain_part = jnp.sum(grad_normed * unit_rows.astype(jnp.float32), axis=0)
    weight_grad, gain_grad = (
        lax.psum_scatter(weight_part, "fsdp", scatter_dimension=0, tiled=True),
        lax.psum_scatter(gain_part, "fsdp", scatter_dimension=0, tiled=True),
    )
    outer_now = lax.dynamic_index_in_dim(outer_params, fragment, 0, keepdims=False)
    momentum_now = lax.dynamic_index_in_dim(outer_momentum, fragment, 0, keepdims=False)
    inner_now = lax.dynamic_index_in_dim(inner_params[0], fragment, 0, keepdims=False).astype(
        jnp.float32
    )
    pseudo_term = outer_now - inner_now
    replica_count = lax.axis_size("replica")
    col_width = outer_now.shape[1] // replica_count
    col_start = lax.axis_index("replica") * col_width
    pseudo_grad = lax.psum(pseudo_term, "replica") / replica_count
    momentum_next = 0.9 * momentum_now + pseudo_grad
    outer_next = outer_now - 0.7 * (pseudo_grad + 0.9 * momentum_next)
    own_outer = lax.dynamic_slice_in_dim(outer_next, col_start, col_width, 1)
    own_momentum = lax.dynamic_slice_in_dim(momentum_next, col_start, col_width, 1)
    mix_alpha = (mix_step[0].astype(jnp.float32) + 1.0) / (MIXSTEPS + 1.0)
    new_inner = (mix_alpha * outer_next + (1.0 - mix_alpha) * inner_now).astype(jnp.bfloat16)
    return (key_out, weight_grad[None], gain_grad[None], own_outer, own_momentum, new_inner[None])


def solution(mesh):
    in_specs = (
        P(("replica", "fsdp"), None),
        P("fsdp"),
        P("fsdp", None),
        P(("replica", "fsdp"), None),
        P(None, "fsdp", None),
        P(None, "fsdp", None),
        P("replica", None, "fsdp", None),
        P(),
        P("replica"),
    )
    out_specs = (
        P(("replica", "fsdp"), None),
        P("replica", "fsdp", None),
        P("replica", "fsdp"),
        P("fsdp", "replica"),
        P("fsdp", "replica"),
        P("replica", "fsdp", None),
    )
    return jax.shard_map(
        on_device, mesh=mesh, in_specs=in_specs, out_specs=out_specs, check_vma=False
    )
```

profile of v0, /device:TPU:8, one launch (start us, length us, event | category | flops | bytes accessed | tf_op | source)
XLA Modules:
  0.0 462.4 jit_solution(5988033657452385782)
XLA Ops:
  7.2 0.0 copy-start
  7.2 0.0 copy-start.1
  7.2 0.0 all-gather.3.cloned.1.call-start
  7.2 0.7 all-gather.3.cloned.1.call-update
  7.9 0.0 reduce-scatter.2.cloned.1.call-start
  8.0 0.7 reshape.77
  8.7 51.7 %all-gather = bf16[16,1,512]{2,1,0:T(2,128)(2,1)S(1)} all-gather(bf16[1,1,512]{2,1,0:T(2,128)(2,1)S(1)} %reshape.77), channel_id=1, replica_groups=mesh['replica'=64,'fsdp'=16] {'fsdp'}, dimensions={0}, use_global_device_ids=true | all-gather | bytes 17408 | tf_op jit(solution)/shard_map/all_gather | solution.py:28
  60.4 2.1 fusion
  62.5 0.0 copy-done
  62.5 0.0 copy-done.1
  62.5 2.7 fusion.3
  65.2 0.0 reduce-scatter.2.cloned.1.call-update
  66.6 1.3 dynamic-slice.1
  68.5 1.0 convert_subtract_fusion
  69.4 282.0 %psum.7 = f32[1,8192]{1,0:T(1,128)S(1)} all-reduce(f32[1,8192]{1,0:T(1,128)S(1)} %convert_subtract_fusion), channel_id=1, replica_groups=mesh['replica'=64,'fsdp'=16] {'replica'}, use_global_device_ids=true, to_apply=%region_4.5 | all-reduce | flops 8192 | bytes 65536 | tf_op jit(solution)/shard_map/psum | solution.py:52
  351.5 1.7 fusion.13
  353.1 0.5 constant_dynamic-slice_fusion
  353.7 0.0 all-gather.3.cloned.1.call-done
  353.7 2.3 fusion.7
  356.0 95.9 %all-reduce = f32[8192]{0:T(1024)S(1)} all-reduce(f32[8192]{0:T(1024)S(1)} %fusion.7), channel_id=3, replica_groups=mesh['replica'=64,'fsdp'=16] {'fsdp'}, use_global_device_ids=true, to_apply=%region_3.0.clone | all-reduce | flops 8192 | bytes 65536
  451.9 0.7 dynamic-slice.2
  452.5 3.0 fusion.8
  455.6 0.0 reduce-scatter.2.cloned.1.call-done
  (2 shorter events, 0.0 us)
Async XLA Ops:
  7.2 55.3 %copy-start = (bf16[128,128]{1,0:T(8,128)(2,1)S(1)}, bf16[128,128]{1,0:T(8,128)(2,1)}, u32[]{:S(2)}) copy-start(bf16[128,128]{1,0:T(8,128)(2,1)} %param.12) | copy-start | bytes 98308
  7.2 55.3 %copy-start.1 = (bf16[128,8192]{1,0:T(8,128)(2,1)S(1)}, bf16[128,8192]{1,0:T(8,128)(2,1)}, u32[]{:S(2)}) copy-start(bf16[128,8192]{1,0:T(8,128)(2,1)} %param.9) | copy-start | bytes 6291460
  7.2 346.5 %all-gather.3.cloned.1.call-start = ((), (), s32[]{:S(2)}) async-start(), calls=%async_computation.1 | async-start | bytes 2228224 | tf_op jit(solution)/shard_map/all_gather | solution.py:27
  7.9 447.6 %reduce-scatter.2.cloned.1.call-start = ((), (), s32[]{:S(2)}) async-start(), calls=%async_computation.2 | async-start | bytes 4456448 | tf_op jit(solution)/shard_map/reduce_scatter | solution.py:40
Sparse Core Ops, SparseCore 0:
  12.4 119.6 all-gather.2
  138.5 242.7 reduce-scatter.1
where the time goes:
time: 463 us; the launch traced here: 462 us
  blocking collectives  430 us (93%)
  between operations  16.1 us (3%)
  matrix products  8.1 us (2%)
  other arithmetic  4.75 us (1%)
    psum x1, blocking collectives, on_device(): pseudo_grad = lax.psum(pseudo_term, 'replica') / replica_count  282 us
    unnamed x1, blocking collectives  95.9 us
    all_gather x1, blocking collectives, on_device(): lax.all_gather(norm_gain, 'fsdp', axis=0, tiled=True)  51.7 us
  transfers between devices with their start and end apart: 2, of which 0 were waited for; matrix products, arithmetic and copies ran while one was open for 3% of the time, Pallas kernels for 0%

commit v1 on v0

v1 whole, which is shorter than its diff:
```python
import jax
import jax.numpy as jnp
from jax import lax
from jax.experimental import pallas as pl
from jax.sharding import PartitionSpec as P


MIXSTEPS = 8
ALL = ("replica", "fsdp")

norm_eps = 1e-05


def route(move):
    pairs = []
    for r in range(64):
        for f in range(16):
            z, y, c, x = r // 8, (r // 2) % 4 + 4 * (f % 2), r % 2, f // 2
            z, y, c, x = move(z, y, c, x)
            pairs.append((r * 16 + f, (z * 8 + y % 4 * 2 + c) * 16 + x * 2 + y // 4))
    return pairs


def permute(value, move):
    return lax.ppermute(value, ALL, route(move))


def other_pair(i, n):
    return (i + 1) % n if i % 2 else (i - 1) % n


def x_near(z, y, c, x):
    return z, y, c, x ^ 1


def x_near_other(z, y, c, x):
    return z, y, c, other_pair(x, 8)


def x_two(z, y, c, x):
    return z, y, c, x ^ 2


def x_four(z, y, c, x):
    return z, y, c, x ^ 4


def y_half(z, y, c, x):
    return z, (6, 7, 4, 5, 2, 3, 0, 1)[y], c, x


def y_one(z, y, c, x):
    return z, y ^ 1, c, x


def y_two(z, y, c, x):
    return z, y ^ 2, c, x


def z_one(z, y, c, x):
    return z ^ 1, y, c, x


def z_two(z, y, c, x):
    return z ^ 2, y, c, x


def z_four(z, y, c, x):
    return z ^ 4, y, c, x


def core_swap(z, y, c, x):
    return z, y, 1 - c, x


def factor_kernel(tok_ref, cot_ref, inv_ref, keep_ref, send_a, send_b):
    tokens, width = tok_ref.shape
    chunk = keep_ref.shape[2]

    def squares(i, acc):
        for k in range(chunk // 128):
            t = tok_ref[:, pl.ds(pl.multiple_of(i * chunk + k * 128, 128), 128)].astype(jnp.float32)
            acc = acc + t * t
        return acc

    acc = lax.fori_loop(0, width // chunk, squares, jnp.zeros((tokens, 128), jnp.float32))
    inv = lax.rsqrt(jnp.sum(acc, axis=1, keepdims=True) / width + norm_eps)
    inv_ref[...] = jnp.broadcast_to(inv, inv_ref.shape)
    scaled = (cot_ref[...].astype(jnp.float32) * inv).T.astype(jnp.bfloat16)
    parity = (lax.axis_index("fsdp") // 2) % 2

    def product(slot, x0):
        source = ((slot // 2) * 2 + x0) * 2 + slot % 2
        columns = tok_ref[:, pl.ds(pl.multiple_of(source * chunk, chunk), chunk)]
        return jnp.dot(scaled, columns, preferred_element_type=jnp.float32).astype(jnp.bfloat16)

    for slot in range(8):
        (send_a, send_b)[slot // 4][slot % 4] = product(slot, 1 - parity)
        keep_ref[slot] = product(slot, parity)


def factor_parts(tokens, cot, chunk):
    hd = cot.shape[1]
    half = jax.ShapeDtypeStruct((4, hd, chunk), jnp.bfloat16)
    return pl.pallas_call(
        factor_kernel,
        out_shape=(
            jax.ShapeDtypeStruct((tokens.shape[0], 128), jnp.float32),
            jax.ShapeDtypeStruct((8, hd, chunk), jnp.bfloat16),
            half,
            half,
        ),
    )(tokens, cot)


def add_kernel(keep_ref, a_ref, b_ref, out_ref):
    for slot in range(8):
        other = (a_ref, b_ref)[slot // 4][slot % 4]
        out_ref[slot] = (keep_ref[slot].astype(jnp.float32) + other.astype(jnp.float32)).astype(
            out_ref.dtype
        )


def add_parts(keep, a, b):
    return pl.pallas_call(
        add_kernel, out_shape=jax.ShapeDtypeStruct(keep.shape, keep.dtype)
    )(keep, a, b)


def keys_product(tok_ref, w_ref, flip):
    shards, rows, hd = w_ref.shape
    core = lax.axis_index("replica") % 2
    half = core + flip - 2 * core * flip
    place = lax.axis_index("fsdp")
    acc = jnp.zeros((tok_ref.shape[0], hd), jnp.float32)
    for slot in range(shards):
        step = (slot // 8) * 2 + (slot // 4 % 2) * 4 + (slot // 2 % 2) + (slot % 2) * 8
        start = pl.multiple_of(((place ^ step) * 2 + half) * rows, rows)
        acc = acc + jnp.dot(
            tok_ref[:, pl.ds(start, rows)], w_ref[slot], preferred_element_type=jnp.float32
        )
    return acc


def keys_first(tok_ref, w_ref, out_ref):
    out_ref[...] = keys_product(tok_ref, w_ref, 0)


def keys_second(tok_ref, w_ref, inv_ref, first_ref, out_ref):
    acc = first_ref[...] + keys_product(tok_ref, w_ref, 1)
    out_ref[...] = (acc * inv_ref[...]).astype(out_ref.dtype)


def step(
    tokens,
    norm_gain,
    key_weight,
    key_cotangent,
    outer_params,
    outer_momentum,
    inner_params,
    fragment,
    mix_step,
):
    rows, hd = key_weight.shape
    replica = lax.axis_index("replica")
    replicas = lax.axis_size("replica")
    core = replica % 2

    inv, keep, send_a, send_b = factor_parts(tokens, key_cotangent, rows)
    recv_a = permute(send_a, x_near)
    recv_b = permute(send_b, x_near_other)

    half = rows // 2
    gain_half = lax.dynamic_slice_in_dim(norm_gain, core * half, half, 0).astype(jnp.float32)
    weight_half = lax.dynamic_slice_in_dim(key_weight, core * half, half, 0).astype(jnp.float32)
    w_half = (gain_half[:, None] * weight_half).astype(jnp.bfloat16)[None]

    def doubled(values, move):
        return jnp.concatenate([values, permute(values, move)])

    w_half = doubled(w_half, x_four)
    w_half = doubled(w_half, y_half)
    part = add_parts(keep, recv_a, recv_b)
    x_groups = [[4 * k + 2 * p + y for k in range(4) for y in range(2)] for p in range(2)]
    mine = lax.all_to_all(part, "fsdp", 0, 0, axis_index_groups=x_groups)
    w_half = doubled(w_half, x_two)
    w_half = doubled(w_half, x_near)

    blocks = (replicas // 2, 2, outer_params.shape[2] // replicas)

    def row_of(values):
        return lax.dynamic_index_in_dim(values, fragment, 0, keepdims=False).reshape(blocks)

    def half_of(values):
        return lax.dynamic_index_in_dim(values, core, 1, keepdims=False)

    inner_row = row_of(inner_params[0])
    other_core = permute(
        lax.dynamic_index_in_dim(inner_row, 1 - core, 1, keepdims=False), core_swap
    )
    total = half_of(inner_row).astype(jnp.float32) + other_core.astype(jnp.float32)
    for move in (y_one, y_two, z_one, z_two, z_four):
        total = total + permute(total, move)
    outer_now = half_of(row_of(outer_params))
    momentum_now = half_of(row_of(outer_momentum))
    pseudo_grad = outer_now - total / replicas
    momentum_next = 0.9 * momentum_now + pseudo_grad
    outer_next = outer_now - 0.7 * (pseudo_grad + 0.9 * momentum_next)
    own_outer = lax.dynamic_slice_in_dim(outer_next, replica // 2, 1, 0)
    own_momentum = lax.dynamic_slice_in_dim(momentum_next, replica // 2, 1, 0)
    outer_other = permute(outer_next, core_swap)
    outer_pair = jnp.where(
        core == 0,
        jnp.stack([outer_next, outer_other], axis=1),
        jnp.stack([outer_other, outer_next], axis=1),
    )
    mix_alpha = (mix_step[0].astype(jnp.float32) + 1.0) / (MIXSTEPS + 1.0)
    new_inner = mix_alpha * outer_pair + (1.0 - mix_alpha) * inner_row.astype(jnp.float32)
    new_inner = new_inner.astype(jnp.bfloat16).reshape(1, -1)

    w_other = permute(w_half, core_swap)
    out = jax.ShapeDtypeStruct((tokens.shape[0], hd), jnp.bfloat16)
    first = pl.pallas_call(
        keys_first, out_shape=jax.ShapeDtypeStruct(out.shape, jnp.float32)
    )(tokens, w_half)
    key_out = pl.pallas_call(keys_second, out_shape=out)(tokens, w_other, inv, first)

    factor = jnp.sum(mine.astype(jnp.float32), axis=0).T
    weight_grad = norm_gain.astype(jnp.float32)[:, None] * factor
    gain_grad = jnp.sum(key_weight.astype(jnp.float32) * factor, axis=1)
    return (key_out, weight_grad[None], gain_grad[None], own_outer, own_momentum, new_inner[None])


def solution(mesh):
    in_specs = (
        P(("replica", "fsdp"), None),
        P("fsdp"),
        P("fsdp", None),
        P(("replica", "fsdp"), None),
        P(None, "fsdp", None),
        P(None, "fsdp", None),
        P("replica", None, "fsdp", None),
        P(),
        P("replica"),
    )
    out_specs = (
        P(("replica", "fsdp"), None),
        P("replica", "fsdp", None),
        P("replica", "fsdp"),
        P("fsdp", "replica"),
        P("fsdp", "replica"),
        P("replica", "fsdp", None),
    )
    return jax.shard_map(step, mesh=mesh, in_specs=in_specs, out_specs=out_specs, check_vma=False)
```

time: 463 us -> 126 us (0.27)
  the two profiles are of different devices: /device:TPU:8 before, /device:TPU:14 now
where the time goes in v1:
time: 126 us; the launch traced here: 125 us
  starting transfers between devices  68.3 us (54%)
  waiting for transfers between devices  31.4 us (25%)
  Pallas kernels  13 us (10%)
  local copies, waits for them, and re-layouts  5.8 us (5%)
  other arithmetic  4.25 us (3%)
  between operations  2.39 us (2%)
    ppermute x14, starting transfers between devices, permute(): return lax.ppermute(value, ALL, route(move))  58.3 us
    all_to_all x1, waiting for transfers between devices, step(): mine = lax.all_to_all(part, 'fsdp', 0, 0, axis_index_groups=x_groups)  18.4 us
    ppermute x14, waiting for transfers between devices, permute(): return lax.ppermute(value, ALL, route(move))  13 us
    all_to_all x1, starting transfers between devices, step(): mine = lax.all_to_all(part, 'fsdp', 0, 0, axis_index_groups=x_groups)  9.94 us
    pallas_call x1, Pallas kernels, factor_parts(): pl.pallas_call(factor_kernel, out_shape=(jax.ShapeDtypeStruct((tokens.sha...  4.34 us
    pallas_call x1, Pallas kernels, step(): pl.pallas_call(keys_second, out_shape=out)(tokens, w_other, inv, first)  2.98 us
    pallas_call x1, Pallas kernels, step(): pl.pallas_call(keys_first, out_shape=jax.ShapeDtypeStruct(out.shape, jnp....  2.92 us
    unnamed x16, local copies, waits for them, and re-layouts  2.82 us
  transfers between devices with their start and end apart: 15, of which 5 were waited for; matrix products, arithmetic and copies ran while one was open for 4% of the time, Pallas kernels for 10%

profile of v1, /device:TPU:14, one launch (start us, length us, event | category | flops | bytes accessed | tf_op | source)
XLA Modules:
  0.0 125.1 jit_solution(16453374477296093525)
XLA Ops:
  0.6 0.0 copy-start.4
  0.6 0.0 copy-start.3
  1.4 1.0 dynamic-slice_reduce_fusion
  2.4 1.9 %collective-permute-start.7 = (bf16[32,128]{1,0:T(8,128)(2,1)S(1)}, bf16[32,128]{1,0:T(8,128)(2,1)S(1)}, u32[]{:S(2)}, u32[]{:S(2)}) collective-permute-start(bf16[32,128]{1,0:T(8,128)(2,1)S(1)} %bitcast.43), channel_id=1, source_target_pairs={{0,16},{1,17},{2,18},{3,19},{4,20},{5,21},{6,22},{7,23},{8,24},{9,... | collective-permute-start | bytes 24584 | tf_op jit(solution)/shard_map/ppermute | solution.py:25
  4.4 0.8 dynamic-slice_convert_fusion.1
  5.1 0.4 collective-permute-done.7
  5.5 3.6 %collective-permute-start.8 = (f32[32,128]{1,0:T(8,128)S(1)}, f32[32,128]{1,0:T(8,128)S(1)}, u32[]{:S(2)}, u32[]{:S(2)}) collective-permute-start(f32[32,128]{1,0:T(8,128)S(1)} %convert_add_fusion), channel_id=1, source_target_pairs={{0,32},{1,33},{2,34},{3,35},{4,36},{5,37},{6,38},{7,39},{8,40},{9,... | collective-permute-start | bytes 49160 | tf_op jit(solution)/shard_map/ppermute | solution.py:25
  9.1 0.9 constant_dynamic-update-slice_fusion.4
  10.1 5.1 %collective-permute-start = (bf16[1,256,128]{2,1,0:T(8,128)(2,1)S(1)}, bf16[1,256,128]{2,1,0:T(8,128)(2,1)S(1)}, u32[]{:S(2)}, u32[]{:S(2)}) collective-permute-start(bf16[1,256,128]{2,1,0:T(8,128)(2,1)S(1)} %get-tuple-element.21), channel_id=1, source_target_pairs={{0,8},{1,9},{2,10},{3,11},{4,12},{5,13},{6,14},{7,15},{8,0},{9,1},... | collective-permute-start | bytes 196616 | tf_op jit(solution)/shard_map/ppermute | solution.py:25
  15.1 4.3 %shard_map.136 = (f32[128,128]{1,0:T(8,128)}, bf16[8,128,512]{2,1,0:T(8,128)(2,1)}, bf16[4,128,512]{2,1,0:T(8,128)(2,1)}, bf16[4,128,512]{2,1,0:T(8,128)(2,1)}) custom-call(bf16[128,8192]{1,0:T(8,128)(2,1)} %tok_ref.5, bf16[128,128]{1,0:T(8,128)(2,1)} %cot_ref.1), custom_call_target="tpu_custom_call" | custom-call | tf_op jit(solution)/shard_map/pallas_call | solution.py:105
  19.5 2.4 %collective-permute-start.5 = (bf16[4,128,512]{2,1,0:T(8,128)(2,1)}, bf16[4,128,512]{2,1,0:T(8,128)(2,1)S(1)}, u32[]{:S(2)}, u32[]{:S(2)}) collective-permute-start(bf16[4,128,512]{2,1,0:T(8,128)(2,1)} %get-tuple-element.12), channel_id=1, source_target_pairs={{0,2},{1,3},{2,0},{3,1},{4,6},{5,7},{6,4},{7,5},{8,10},{9,11},{10,... | collective-permute-start | bytes 1572872 | tf_op jit(solution)/shard_map/ppermute | solution.py:25
  21.9 9.6 %collective-permute-start.6 = (bf16[4,128,512]{2,1,0:T(8,128)(2,1)}, bf16[4,128,512]{2,1,0:T(8,128)(2,1)}, u32[]{:S(2)}, u32[]{:S(2)}) collective-permute-start(bf16[4,128,512]{2,1,0:T(8,128)(2,1)} %get-tuple-element.13), channel_id=1, source_target_pairs={{0,14},{1,15},{2,4},{3,5},{4,2},{5,3},{6,8},{7,9},{8,6},{9,7},{10,... | collective-permute-start | bytes 1572872 | tf_op jit(solution)/shard_map/ppermute | solution.py:25
  31.5 0.0 collective-permute-done.8
  31.5 1.9 %collective-permute-start.9 = (f32[32,128]{1,0:T(8,128)S(1)}, f32[32,128]{1,0:T(8,128)S(1)}, u32[]{:S(2)}, u32[]{:S(2)}) collective-permute-start(f32[32,128]{1,0:T(8,128)S(1)} %add.75), channel_id=1, source_target_pairs={{0,64},{1,65},{2,66},{3,67},{4,68},{5,69},{6,70},{7,71},{8,72},{9,... | collective-permute-start | bytes 49160 | tf_op jit(solution)/shard_map/ppermute | solution.py:25
  33.4 0.8 constant_dynamic-slice_fusion.3
  34.2 3.8 %collective-permute-done.9 = f32[32,128]{1,0:T(8,128)S(1)} collective-permute-done((f32[32,128]{1,0:T(8,128)S(1)}, f32[32,128]{1,0:T(8,128)S(1)}, u32[]{:S(2)}, u32[]{:S(2)}) %collective-permute-start.9) | collective-permute-done | bytes 16416 | tf_op jit(solution)/shard_map/ppermute | solution.py:25
  38.0 1.9 %collective-permute-start.10 = (f32[32,128]{1,0:T(8,128)S(1)}, f32[32,128]{1,0:T(8,128)S(1)}, u32[]{:S(2)}, u32[]{:S(2)}) collective-permute-start(f32[32,128]{1,0:T(8,128)S(1)} %add.76), channel_id=1, source_target_pairs={{0,128},{1,129},{2,130},{3,131},{4,132},{5,133},{6,134},{7,135},{8... | collective-permute-start | bytes 49160 | tf_op jit(solution)/shard_map/ppermute | solution.py:25
  40.0 0.0 collective-permute-done
  40.0 4.3 %collective-permute-start.1 = (bf16[2,256,128]{2,1,0:T(8,128)(2,1)S(1)}, bf16[2,256,128]{2,1,0:T(8,128)(2,1)S(1)}, u32[]{:S(2)}, u32[]{:S(2)}) collective-permute-start(bf16[2,256,128]{2,1,0:T(8,128)(2,1)S(1)} %pad_maximum_fusion.2), channel_id=1, source_target_pairs={{0,65},{1,64},{2,67},{3,66},{4,69},{5,68},{6,71},{7,70},{8,73},{9,... | collective-permute-start | bytes 393224 | tf_op jit(solution)/shard_map/ppermute | solution.py:25
  44.3 0.0 collective-permute-done.10
  44.4 7.9 %collective-permute-start.11 = (f32[32,128]{1,0:T(8,128)S(1)}, f32[32,128]{1,0:T(8,128)S(1)}, u32[]{:S(2)}, u32[]{:S(2)}) collective-permute-start(f32[32,128]{1,0:T(8,128)S(1)} %add.77), channel_id=1, source_target_pairs={{0,256},{1,257},{2,258},{3,259},{4,260},{5,261},{6,262},{7,263},{8... | collective-permute-start | bytes 49160 | tf_op jit(solution)/shard_map/ppermute | solution.py:25
  52.3 0.1 copy.19
  53.1 0.8 collective-permute-done.11
  54.0 11.9 %collective-permute-start.12 = (f32[32,128]{1,0:T(8,128)S(1)}, f32[32,128]{1,0:T(8,128)S(1)}, u32[]{:S(2)}, u32[]{:S(2)}) collective-permute-start(f32[32,128]{1,0:T(8,128)S(1)} %add.78), channel_id=1, source_target_pairs={{0,512},{1,513},{2,514},{3,515},{4,516},{5,517},{6,518},{7,519},{8... | collective-permute-start | bytes 49160 | tf_op jit(solution)/shard_map/ppermute | solution.py:25
  65.8 0.0 collective-permute-done.1
  65.9 2.1 %collective-permute-start.2 = (bf16[4,256,128]{2,1,0:T(8,128)(2,1)S(1)}, bf16[4,256,128]{2,1,0:T(8,128)(2,1)S(1)}, u32[]{:S(2)}, u32[]{:S(2)}) collective-permute-start(bf16[4,256,128]{2,1,0:T(8,128)(2,1)S(1)} %pad_maximum_fusion.1), channel_id=1, source_target_pairs={{0,4},{1,5},{2,6},{3,7},{4,0},{5,1},{6,2},{7,3},{8,12},{9,13},{10,... | collective-permute-start | bytes 786440 | tf_op jit(solution)/shard_map/ppermute | solution.py:25
  68.0 0.0 collective-permute-done.12
  68.0 1.9 %collective-permute-start.13 = (f32[32,128]{1,0:T(8,128)S(1)}, f32[32,128]{1,0:T(8,128)S(1)}, u32[]{:S(2)}, u32[]{:S(2)}) collective-permute-start(f32[32,128]{1,0:T(8,128)S(1)} %get-tuple-element.25), channel_id=1, source_target_pairs={{0,16},{1,17},{2,18},{3,19},{4,20},{5,21},{6,22},{7,23},{8,24},{9,... | collective-permute-start | bytes 49160 | tf_op jit(solution)/shard_map/ppermute | solution.py:25
  70.0 8.0 %collective-permute-done.2 = bf16[4,256,128]{2,1,0:T(8,128)(2,1)S(1)} collective-permute-done((bf16[4,256,128]{2,1,0:T(8,128)(2,1)S(1)}, bf16[4,256,128]{2,1,0:T(8,128)(2,1)S(1)}, u32[]{:S(2)}, u32[]{:S(2)}) %collective-permute-start.2) | collective-permute-done | bytes 262176 | tf_op jit(solution)/shard_map/ppermute | solution.py:25
  78.0 0.1 pad_maximum_fusion
  78.0 1.9 %collective-permute-start.3 = (bf16[8,256,128]{2,1,0:T(8,128)(2,1)S(1)}, bf16[8,256,128]{2,1,0:T(8,128)(2,1)S(1)}, u32[]{:S(2)}, u32[]{:S(2)}) collective-permute-start(bf16[8,256,128]{2,1,0:T(8,128)(2,1)S(1)} %pad_maximum_fusion), channel_id=1, source_target_pairs={{0,2},{1,3},{2,0},{3,1},{4,6},{5,7},{6,4},{7,5},{8,10},{9,11},{10,... | collective-permute-start | bytes 1572872 | tf_op jit(solution)/shard_map/ppermute | solution.py:25
  79.9 0.5 constant_dynamic-slice_fusion.1
  80.5 0.5 constant_dynamic-slice_fusion
  81.1 0.0 collective-permute-done.5.a_ref
  81.1 0.8 copy-done.2
  81.9 2.7 %shard_map.139 = bf16[8,128,512]{2,1,0:T(8,128)(2,1)} custom-call(bf16[8,128,512]{2,1,0:T(8,128)(2,1)} %get-tuple-element.11.keep_ref, bf16[4,128,512]{2,1,0:T(8,128)(2,1)} %copy-done.2, bf16[4,128,512]{2,1,0:T(8,128)(2,1)} %collective-permute-done.6.b_ref), custom_call_target="tpu_custom_call" | custom-call | tf_op jit(solution)/shard_map/pallas_call | solution.py:125
  84.6 9.9 %all-to-all-start = ((bf16[8,128,512]{2,1,0:T(8,128)(2,1)}), bf16[8,128,512]{2,1,0:T(8,128)(2,1)S(1)}, u32[]{:S(2)}, u32[]{:S(2)}) async-start(bf16[8,128,512]{2,1,0:T(8,128)(2,1)} %shard_map.139), calls=%async_computation | async-start | bytes 2097152 | tf_op jit(solution)/shard_map/all_to_all | solution.py:186
  94.6 0.0 collective-permute-done.3
  94.6 0.1 constant_dynamic-update-slice_fusion.w_ref
  94.7 1.9 %collective-permute-start.4 = (bf16[16,256,128]{2,1,0:T(8,128)(2,1)S(1)}, bf16[16,256,128]{2,1,0:T(8,128)(2,1)S(1)}, u32[]{:S(2)}, u32[]{:S(2)}) collective-permute-start(bf16[16,256,128]{2,1,0:T(8,128)(2,1)S(1)} %constant_dynamic-update-slice_fusion.w_ref), channel_id=1, source_target_pairs={{0,16},{1,17},{2,18},{3,19},{4,20},{5,21},{6,22},{7,23},{8,24},{9,... | collective-permute-start | bytes 3145736 | tf_op jit(solution)/shard_map/ppermute | solution.py:25
  96.6 1.6 %fusion.4 = bf16[1,1,8192]{2,1,0:T(2,128)(2,1)} fusion(f32[1,1,8192]{2,1,0:T(1,128)S(1)} %bitcast.35, bf16[1,32,1,8192]{3,1,2,0:T(8,128)(2,1)} %param.15, s32[]{:T(128)S(6)} %select_n.55, f32[]{:T(128)S(6)} %sub.21), kind=kLoop, calls=%fused_computation.13 | loop fusion | flops 32768 | bytes 65544 | tf_op jit(solution)/shard_map/convert_element_type | solution.py:220
  98.2 2.9 %shard_map.137.first_ref = f32[128,128]{1,0:T(8,128)} custom-call(bf16[128,8192]{1,0:T(8,128)(2,1)} %tok_ref.5, bf16[16,256,128]{2,1,0:T(8,128)(2,1)} %copy-done), custom_call_target="tpu_custom_call" | custom-call | tf_op jit(solution)/shard_map/pallas_call | solution.py:224
  101.1 1.0 copy-done.1
  102.1 3.0 %shard_map.138 = bf16[128,128]{1,0:T(8,128)(2,1)} custom-call(bf16[128,8192]{1,0:T(8,128)(2,1)} %tok_ref.5, bf16[16,256,128]{2,1,0:T(8,128)(2,1)} %copy-done.1, f32[128,128]{1,0:T(8,128)} %get-tuple-element.10.inv_ref, f32[128,128]{1,0:T(8,128)} %shard_map.137.first_ref), custom_call_target="tpu_custom_call" | custom-call | tf_op jit(solution)/shard_map/pallas_call | solution.py:227
  105.1 18.4 %all-to-all-done = bf16[8,128,512]{2,1,0:T(8,128)(2,1)S(1)} async-done(((bf16[8,128,512]{2,1,0:T(8,128)(2,1)}), bf16[8,128,512]{2,1,0:T(8,128)(2,1)S(1)}, u32[]{:S(2)}, u32[]{:S(2)}) %all-to-all-start) | async-done | bytes 1048608 | tf_op jit(solution)/shard_map/all_to_all | solution.py:186
  123.5 0.1 convert_reduce_fusion
  123.6 0.6 fusion.1
  124.3 0.8 copy.22
  (27 shorter events, 0.3 us)
Async XLA Ops:
  0.6 51.8 %copy-start.4 = (bf16[512]{0:T(512)(128)(2,1)S(1)}, bf16[512]{0:T(512)(128)(2,1)}, u32[]{:S(2)}) copy-start(bf16[512]{0:T(512)(128)(2,1)} %param.10) | copy-start | bytes 3076
  0.6 51.7 %copy-start.3 = (bf16[512,128]{1,0:T(8,128)(2,1)S(1)}, bf16[512,128]{1,0:T(8,128)(2,1)}, u32[]{:S(2)}) copy-start(bf16[512,128]{1,0:T(8,128)(2,1)} %param.11) | copy-start | bytes 393220
  2.4 3.1 %collective-permute-start.7 = (bf16[32,128]{1,0:T(8,128)(2,1)S(1)}, bf16[32,128]{1,0:T(8,128)(2,1)S(1)}, u32[]{:S(2)}, u32[]{:S(2)}) collective-permute-start(bf16[32,128]{1,0:T(8,128)(2,1)S(1)} %bitcast.43), channel_id=1, source_target_pairs={{0,16},{1,17},{2,18},{3,19},{4,20},{5,21},{6,22},{7,23},{8,24},{9,... | collective-permute-start | bytes 24584 | tf_op jit(solution)/shard_map/ppermute | solution.py:25
  5.5 26.0 %collective-permute-start.8 = (f32[32,128]{1,0:T(8,128)S(1)}, f32[32,128]{1,0:T(8,128)S(1)}, u32[]{:S(2)}, u32[]{:S(2)}) collective-permute-start(f32[32,128]{1,0:T(8,128)S(1)} %convert_add_fusion), channel_id=1, source_target_pairs={{0,32},{1,33},{2,34},{3,35},{4,36},{5,37},{6,38},{7,39},{8,40},{9,... | collective-permute-start | bytes 49160 | tf_op jit(solution)/shard_map/ppermute | solution.py:25
  10.1 29.9 %collective-permute-start = (bf16[1,256,128]{2,1,0:T(8,128)(2,1)S(1)}, bf16[1,256,128]{2,1,0:T(8,128)(2,1)S(1)}, u32[]{:S(2)}, u32[]{:S(2)}) collective-permute-start(bf16[1,256,128]{2,1,0:T(8,128)(2,1)S(1)} %get-tuple-element.21), channel_id=1, source_target_pairs={{0,8},{1,9},{2,10},{3,11},{4,12},{5,13},{6,14},{7,15},{8,0},{9,1},... | collective-permute-start | bytes 196616 | tf_op jit(solution)/shard_map/ppermute | solution.py:25
  19.5 61.6 %collective-permute-start.5 = (bf16[4,128,512]{2,1,0:T(8,128)(2,1)}, bf16[4,128,512]{2,1,0:T(8,128)(2,1)S(1)}, u32[]{:S(2)}, u32[]{:S(2)}) collective-permute-start(bf16[4,128,512]{2,1,0:T(8,128)(2,1)} %get-tuple-element.12), channel_id=1, source_target_pairs={{0,2},{1,3},{2,0},{3,1},{4,6},{5,7},{6,4},{7,5},{8,10},{9,11},{10,... | collective-permute-start | bytes 1572872 | tf_op jit(solution)/shard_map/ppermute | solution.py:25
  21.9 59.2 %collective-permute-start.6 = (bf16[4,128,512]{2,1,0:T(8,128)(2,1)}, bf16[4,128,512]{2,1,0:T(8,128)(2,1)}, u32[]{:S(2)}, u32[]{:S(2)}) collective-permute-start(bf16[4,128,512]{2,1,0:T(8,128)(2,1)} %get-tuple-element.13), channel_id=1, source_target_pairs={{0,14},{1,15},{2,4},{3,5},{4,2},{5,3},{6,8},{7,9},{8,6},{9,7},{10,... | collective-permute-start | bytes 1572872 | tf_op jit(solution)/shard_map/ppermute | solution.py:25
  31.5 6.5 %collective-permute-start.9 = (f32[32,128]{1,0:T(8,128)S(1)}, f32[32,128]{1,0:T(8,128)S(1)}, u32[]{:S(2)}, u32[]{:S(2)}) collective-permute-start(f32[32,128]{1,0:T(8,128)S(1)} %add.75), channel_id=1, source_target_pairs={{0,64},{1,65},{2,66},{3,67},{4,68},{5,69},{6,70},{7,71},{8,72},{9,... | collective-permute-start | bytes 49160 | tf_op jit(solution)/shard_map/ppermute | solution.py:25
  38.0 6.3 %collective-permute-start.10 = (f32[32,128]{1,0:T(8,128)S(1)}, f32[32,128]{1,0:T(8,128)S(1)}, u32[]{:S(2)}, u32[]{:S(2)}) collective-permute-start(f32[32,128]{1,0:T(8,128)S(1)} %add.76), channel_id=1, source_target_pairs={{0,128},{1,129},{2,130},{3,131},{4,132},{5,133},{6,134},{7,135},{8... | collective-permute-start | bytes 49160 | tf_op jit(solution)/shard_map/ppermute | solution.py:25
  40.0 25.9 %collective-permute-start.1 = (bf16[2,256,128]{2,1,0:T(8,128)(2,1)S(1)}, bf16[2,256,128]{2,1,0:T(8,128)(2,1)S(1)}, u32[]{:S(2)}, u32[]{:S(2)}) collective-permute-start(bf16[2,256,128]{2,1,0:T(8,128)(2,1)S(1)} %pad_maximum_fusion.2), channel_id=1, source_target_pairs={{0,65},{1,64},{2,67},{3,66},{4,69},{5,68},{6,71},{7,70},{8,73},{9,... | collective-permute-start | bytes 393224 | tf_op jit(solution)/shard_map/ppermute | solution.py:25
  44.4 9.6 %collective-permute-start.11 = (f32[32,128]{1,0:T(8,128)S(1)}, f32[32,128]{1,0:T(8,128)S(1)}, u32[]{:S(2)}, u32[]{:S(2)}) collective-permute-start(f32[32,128]{1,0:T(8,128)S(1)} %add.77), channel_id=1, source_target_pairs={{0,256},{1,257},{2,258},{3,259},{4,260},{5,261},{6,262},{7,263},{8... | collective-permute-start | bytes 49160 | tf_op jit(solution)/shard_map/ppermute | solution.py:25
  54.0 14.0 %collective-permute-start.12 = (f32[32,128]{1,0:T(8,128)S(1)}, f32[32,128]{1,0:T(8,128)S(1)}, u32[]{:S(2)}, u32[]{:S(2)}) collective-permute-start(f32[32,128]{1,0:T(8,128)S(1)} %add.78), channel_id=1, source_target_pairs={{0,512},{1,513},{2,514},{3,515},{4,516},{5,517},{6,518},{7,519},{8... | collective-permute-start | bytes 49160 | tf_op jit(solution)/shard_map/ppermute | solution.py:25
  65.9 12.1 %collective-permute-start.2 = (bf16[4,256,128]{2,1,0:T(8,128)(2,1)S(1)}, bf16[4,256,128]{2,1,0:T(8,128)(2,1)S(1)}, u32[]{:S(2)}, u32[]{:S(2)}) collective-permute-start(bf16[4,256,128]{2,1,0:T(8,128)(2,1)S(1)} %pad_maximum_fusion.1), channel_id=1, source_target_pairs={{0,4},{1,5},{2,6},{3,7},{4,0},{5,1},{6,2},{7,3},{8,12},{9,13},{10,... | collective-permute-start | bytes 786440 | tf_op jit(solution)/shard_map/ppermute | solution.py:25
  68.0 12.9 %collective-permute-start.13 = (f32[32,128]{1,0:T(8,128)S(1)}, f32[32,128]{1,0:T(8,128)S(1)}, u32[]{:S(2)}, u32[]{:S(2)}) collective-permute-start(f32[32,128]{1,0:T(8,128)S(1)} %get-tuple-element.25), channel_id=1, source_target_pairs={{0,16},{1,17},{2,18},{3,19},{4,20},{5,21},{6,22},{7,23},{8,24},{9,... | collective-permute-start | bytes 49160 | tf_op jit(solution)/shard_map/ppermute | solution.py:25
  78.0 16.6 %collective-permute-start.3 = (bf16[8,256,128]{2,1,0:T(8,128)(2,1)S(1)}, bf16[8,256,128]{2,1,0:T(8,128)(2,1)S(1)}, u32[]{:S(2)}, u32[]{:S(2)}) collective-permute-start(bf16[8,256,128]{2,1,0:T(8,128)(2,1)S(1)} %pad_maximum_fusion), channel_id=1, source_target_pairs={{0,2},{1,3},{2,0},{3,1},{4,6},{5,7},{6,4},{7,5},{8,10},{9,11},{10,... | collective-permute-start | bytes 1572872 | tf_op jit(solution)/shard_map/ppermute | solution.py:25
  81.1 0.8 copy-start.2
  84.6 38.8 %all-to-all-start = ((bf16[8,128,512]{2,1,0:T(8,128)(2,1)}), bf16[8,128,512]{2,1,0:T(8,128)(2,1)S(1)}, u32[]{:S(2)}, u32[]{:S(2)}) async-start(bf16[8,128,512]{2,1,0:T(8,128)(2,1)} %shard_map.139), calls=%async_computation | async-start | bytes 2097152 | tf_op jit(solution)/shard_map/all_to_all | solution.py:186
  94.7 3.5 %copy-start = (bf16[16,256,128]{2,1,0:T(8,128)(2,1)}, bf16[16,256,128]{2,1,0:T(8,128)(2,1)S(1)}, u32[]{:S(2)}) copy-start(bf16[16,256,128]{2,1,0:T(8,128)(2,1)S(1)} %constant_dynamic-update-slice_fusion.w_ref) | copy-start | bytes 3145732
  94.7 6.4 %collective-permute-start.4 = (bf16[16,256,128]{2,1,0:T(8,128)(2,1)S(1)}, bf16[16,256,128]{2,1,0:T(8,128)(2,1)S(1)}, u32[]{:S(2)}, u32[]{:S(2)}) collective-permute-start(bf16[16,256,128]{2,1,0:T(8,128)(2,1)S(1)} %constant_dynamic-update-slice_fusion.w_ref), channel_id=1, source_target_pairs={{0,16},{1,17},{2,18},{3,19},{4,20},{5,21},{6,22},{7,23},{8,24},{9,... | collective-permute-start | bytes 3145736 | tf_op jit(solution)/shard_map/ppermute | solution.py:25
  101.1 1.0 copy-start.1

commit v2 on v1

--- a/solution.py
+++ b/solution.py
@@ -2,13 +2,19 @@
 import jax.numpy as jnp
 from jax import lax
 from jax.experimental import pallas as pl
+from jax.experimental.pallas import tpu as pltpu
 from jax.sharding import PartitionSpec as P
 
 
 MIXSTEPS = 8
 ALL = ("replica", "fsdp")
+VMEM = pl.BlockSpec(memory_space=pltpu.VMEM)
 
 norm_eps = 1e-05
+
+
+def on_chip(*values):
+    return [pltpu.with_memory_space_constraint(v, pltpu.VMEM) for v in values]
 
 
 def route(move):
@@ -35,18 +41,6 @@
 
 def x_near_other(z, y, c, x):
     return z, y, c, other_pair(x, 8)
-
-
-def x_two(z, y, c, x):
-    return z, y, c, x ^ 2
-
-
-def x_four(z, y, c, x):
-    return z, y, c, x ^ 4
-
-
-def y_half(z, y, c, x):
-    return z, (6, 7, 4, 5, 2, 3, 0, 1)[y], c, x
 
 
 def y_one(z, y, c, x):
@@ -110,6 +104,8 @@
             half,
             half,
         ),
+        in_specs=[VMEM] * 2,
+        out_specs=(VMEM,) * 4,
     )(tokens, cot)
 
 
@@ -123,31 +119,37 @@
 
 def add_parts(keep, a, b):
     return pl.pallas_call(
-        add_kernel, out_shape=jax.ShapeDtypeStruct(keep.shape, keep.dtype)
-    )(keep, a, b)
-
-
-def keys_product(tok_ref, w_ref, flip):
-    shards, rows, hd = w_ref.shape
-    core = lax.axis_index("replica") % 2
-    half = core + flip - 2 * core * flip
-    place = lax.axis_index("fsdp")
+        add_kernel,
+        out_shape=jax.ShapeDtypeStruct(keep.shape, keep.dtype),
+        in_specs=[VMEM] * 3,
+        out_specs=VMEM,
+    )(*on_chip(keep, a, b))
+
+
+def keys_product(tok_ref, w_refs, flip):
+    groups, shards, piece, hd = w_refs[0].shape
+    rows = groups * piece
+    replica = lax.axis_index("replica")
+    half = (replica + flip) % 2
     acc = jnp.zeros((tok_ref.shape[0], hd), jnp.float32)
-    for slot in range(shards):
-        step = (slot // 8) * 2 + (slot // 4 % 2) * 4 + (slot // 2 % 2) + (slot % 2) * 8
-        start = pl.multiple_of(((place ^ step) * 2 + half) * rows, rows)
-        acc = acc + jnp.dot(
-            tok_ref[:, pl.ds(start, rows)], w_ref[slot], preferred_element_type=jnp.float32
-        )
+    for f in range(shards):
+        for other, w_ref in enumerate(w_refs):
+            quarter = (replica // 8 + other) % 2
+            start = pl.multiple_of(((f * 2 + half) * 2 + quarter) * rows, rows)
+            acc = acc + jnp.dot(
+                tok_ref[:, pl.ds(start, rows)],
+                w_ref[:, f].reshape(rows, hd),
+                preferred_element_type=jnp.float32,
+            )
     return acc
 
 
-def keys_first(tok_ref, w_ref, out_ref):
-    out_ref[...] = keys_product(tok_ref, w_ref, 0)
-
-
-def keys_second(tok_ref, w_ref, inv_ref, first_ref, out_ref):
-    acc = first_ref[...] + keys_product(tok_ref, w_ref, 1)
+def keys_first(tok_ref, near_ref, far_ref, out_ref):
+    out_ref[...] = keys_product(tok_ref, (near_ref, far_ref), 0)
+
+
+def keys_second(tok_ref, near_ref, far_ref, inv_ref, first_ref, out_ref):
+    acc = first_ref[...] + keys_product(tok_ref, (near_ref, far_ref), 1)
     out_ref[...] = (acc * inv_ref[...]).astype(out_ref.dtype)
 
 
@@ -171,21 +173,32 @@
     recv_a = permute(send_a, x_near)
     recv_b = permute(send_b, x_near_other)
 
-    half = rows // 2
-    gain_half = lax.dynamic_slice_in_dim(norm_gain, core * half, half, 0).astype(jnp.float32)
-    weight_half = lax.dynamic_slice_in_dim(key_weight, core * half, half, 0).astype(jnp.float32)
-    w_half = (gain_half[:, None] * weight_half).astype(jnp.bfloat16)[None]
-
-    def doubled(values, move):
-        return jnp.concatenate([values, permute(values, move)])
-
-    w_half = doubled(w_half, x_four)
-    w_half = doubled(w_half, y_half)
+    plane = replica // 8
+    piece = rows // 16
+    z_bits = (plane // 4, plane // 2 % 2, plane % 2)
+    order = core * 8 + z_bits[2] * 4 + z_bits[1] * 2 + z_bits[0]
+    gain_piece = lax.dynamic_slice_in_dim(norm_gain, order * piece, piece, 0).astype(jnp.float32)
+    weight_piece = lax.dynamic_slice_in_dim(key_weight, order * piece, piece, 0).astype(jnp.float32)
+    scaled_piece = (gain_piece[:, None] * weight_piece).astype(jnp.bfloat16)
+    shards = lax.axis_size("fsdp")
+    w_pieces = lax.all_to_all(
+        jnp.broadcast_to(scaled_piece[None], (shards, piece, hd)), "fsdp", 0, 0
+    )[None]
+
+    def doubled(values, move, bit):
+        other = permute(values, move)
+        return jnp.concatenate(
+            [jnp.where(bit == 0, values, other), jnp.where(bit == 0, other, values)]
+        )
+
+    w_pieces = doubled(w_pieces, z_four, z_bits[0])
+    w_near = doubled(w_pieces, z_two, z_bits[1])
+    w_far = permute(w_near, z_one)
+    w_near_other = permute(w_near, core_swap)
+    w_far_other = permute(w_far, core_swap)
     part = add_parts(keep, recv_a, recv_b)
     x_groups = [[4 * k + 2 * p + y for k in range(4) for y in range(2)] for p in range(2)]
     mine = lax.all_to_all(part, "fsdp", 0, 0, axis_index_groups=x_groups)
-    w_half = doubled(w_half, x_two)
-    w_half = doubled(w_half, x_near)
 
     blocks = (replicas // 2, 2, outer_params.shape[2] // replicas)
 
@@ -219,12 +232,16 @@
     new_inner = mix_alpha * outer_pair + (1.0 - mix_alpha) * inner_row.astype(jnp.float32)
     new_inner = new_inner.astype(jnp.bfloat16).reshape(1, -1)
 
-    w_other = permute(w_half, core_swap)
     out = jax.ShapeDtypeStruct((tokens.shape[0], hd), jnp.bfloat16)
     first = pl.pallas_call(
-        keys_first, out_shape=jax.ShapeDtypeStruct(out.shape, jnp.float32)
-    )(tokens, w_half)
-    key_out = pl.pallas_call(keys_second, out_shape=out)(tokens, w_other, inv, first)
+        keys_first,
+        out_shape=jax.ShapeDtypeStruct(out.shape, jnp.float32),
+        in_specs=[VMEM] * 3,
+        out_specs=VMEM,
+    )(tokens, *on_chip(w_near, w_far))
+    key_out = pl.pallas_call(
+        keys_second, out_shape=out, in_specs=[VMEM] * 5, out_specs=VMEM
+    )(tokens, *on_chip(w_near_other, w_far_other, inv, first))
 
     factor = jnp.sum(mine.astype(jnp.float32), axis=0).T
     weight_grad = norm_gain.astype(jnp.float32)[:, None] * factor

time: 126 us -> 137 us (1.087)
  the two profiles are of different devices: /device:TPU:14 before, /device:TPU:32 now
where the time goes in v2:
time: 137 us; the launch traced here: 136 us
  starting transfers between devices  66.7 us (49%)
  waiting for transfers between devices  45.4 us (33%)
  Pallas kernels  10.9 us (8%)
  other arithmetic  5.44 us (4%)
  local copies, waits for them, and re-layouts  5.38 us (4%)
  between operations  2.41 us (2%)
    ppermute x14, starting transfers between devices, permute(): return lax.ppermute(value, ALL, route(move))  50.9 us
    all_to_all x1, waiting for transfers between devices, step(): mine = lax.all_to_all(part, 'fsdp', 0, 0, axis_index_groups=x_groups)  21.8 us
    ppermute x14, waiting for transfers between devices, permute(): return lax.ppermute(value, ALL, route(move))  13.7 us
    all_to_all x1, starting transfers between devices, step(): lax.all_to_all(jnp.broadcast_to(scaled_piece[None], (shards, piece, hd)),...  10.9 us
    all_to_all x1, waiting for transfers between devices, step(): lax.all_to_all(jnp.broadcast_to(scaled_piece[None], (shards, piece, hd)),...  9.87 us
    all_to_all x1, starting transfers between devices, step(): mine = lax.all_to_all(part, 'fsdp', 0, 0, axis_index_groups=x_groups)  4.9 us
    pallas_call x1, Pallas kernels, factor_parts(): pl.pallas_call(factor_kernel, out_shape=(jax.ShapeDtypeStruct((tokens.sha...  4.35 us
  transfers between devices with their start and end apart: 16, of which 5 were waited for; matrix products, arithmetic and copies ran while one was open for 4% of the time, Pallas kernels for 8%

profile of v2, /device:TPU:32, one launch (start us, length us, event | category | flops | bytes accessed | tf_op | source)
XLA Modules:
  0.0 136.2 jit_solution(12815983139082755276)
XLA Ops:
  0.7 0.8 dynamic-slice_convert_fusion.1
  1.5 0.8 multiply_convert_fusion
  2.3 0.7 broadcast_in_dim.8
  3.0 10.9 %all-to-all-start = ((bf16[16,32,128]{2,1,0:T(8,128)(2,1)}), bf16[16,32,128]{2,1,0:T(8,128)(2,1)S(1)}, u32[]{:S(2)}, u32[]{:S(2)}) async-start(bf16[16,32,128]{2,1,0:T(8,128)(2,1)} %broadcast_in_dim.8), calls=%async_computation | async-start | bytes 262144 | tf_op jit(solution)/shard_map/all_to_all | solution.py:184
  14.6 1.0 dynamic-slice_reduce_fusion
  15.7 1.9 %collective-permute-start.7 = (bf16[32,128]{1,0:T(8,128)(2,1)S(1)}, bf16[32,128]{1,0:T(8,128)(2,1)S(1)}, u32[]{:S(2)}, u32[]{:S(2)}) collective-permute-start(bf16[32,128]{1,0:T(8,128)(2,1)S(1)} %bitcast.44), channel_id=1, source_target_pairs={{0,16},{1,17},{2,18},{3,19},{4,20},{5,21},{6,22},{7,23},{8,24},{9,... | collective-permute-start | bytes 24584 | tf_op jit(solution)/shard_map/ppermute | solution.py:31
  17.6 9.9 %all-to-all-done = bf16[16,32,128]{2,1,0:T(8,128)(2,1)S(1)} async-done(((bf16[16,32,128]{2,1,0:T(8,128)(2,1)}), bf16[16,32,128]{2,1,0:T(8,128)(2,1)S(1)}, u32[]{:S(2)}, u32[]{:S(2)}) %all-to-all-start) | async-done | bytes 131104 | tf_op jit(solution)/shard_map/all_to_all | solution.py:184
  27.5 14.5 %collective-permute-start = (bf16[1,16,32,128]{3,2,1,0:T(8,128)(2,1)S(1)}, bf16[1,16,32,128]{3,2,1,0:T(8,128)(2,1)S(1)}, u32[]{:S(2)}, u32[]{:S(2)}) collective-permute-start(bf16[1,16,32,128]{3,2,1,0:T(8,128)(2,1)S(1)} %bitcast.34), channel_id=1, source_target_pairs={{0,512},{1,513},{2,514},{3,515},{4,516},{5,517},{6,518},{7,519},{8... | collective-permute-start | bytes 393224 | tf_op jit(solution)/shard_map/ppermute | solution.py:31
  42.0 0.0 collective-permute-done.7
  42.0 2.7 %collective-permute-start.8 = (f32[32,128]{1,0:T(8,128)S(1)}, f32[32,128]{1,0:T(8,128)S(1)}, u32[]{:S(2)}, u32[]{:S(2)}) collective-permute-start(f32[32,128]{1,0:T(8,128)S(1)} %convert_add_fusion), channel_id=1, source_target_pairs={{0,32},{1,33},{2,34},{3,35},{4,36},{5,37},{6,38},{7,39},{8,40},{9,... | collective-permute-start | bytes 49160 | tf_op jit(solution)/shard_map/ppermute | solution.py:31
  44.7 4.3 %shard_map.136 = (f32[128,128]{1,0:T(8,128)}, bf16[8,128,512]{2,1,0:T(8,128)(2,1)}, bf16[4,128,512]{2,1,0:T(8,128)(2,1)}, bf16[4,128,512]{2,1,0:T(8,128)(2,1)}) custom-call(bf16[128,8192]{1,0:T(8,128)(2,1)} %tok_ref.5, bf16[128,128]{1,0:T(8,128)(2,1)} %cot_ref.1), custom_call_target="tpu_custom_call" | custom-call | tf_op jit(solution)/shard_map/pallas_call | solution.py:99
  49.1 2.4 %collective-permute-start.5 = (bf16[4,128,512]{2,1,0:T(8,128)(2,1)}, bf16[4,128,512]{2,1,0:T(8,128)(2,1)S(1)}, u32[]{:S(2)}, u32[]{:S(2)}) collective-permute-start(bf16[4,128,512]{2,1,0:T(8,128)(2,1)} %get-tuple-element.12), channel_id=1, source_target_pairs={{0,2},{1,3},{2,0},{3,1},{4,6},{5,7},{6,4},{7,5},{8,10},{9,11},{10,... | collective-permute-start | bytes 1572872 | tf_op jit(solution)/shard_map/ppermute | solution.py:31
  51.5 2.8 %collective-permute-start.6 = (bf16[4,128,512]{2,1,0:T(8,128)(2,1)}, bf16[4,128,512]{2,1,0:T(8,128)(2,1)S(1)}, u32[]{:S(2)}, u32[]{:S(2)}) collective-permute-start(bf16[4,128,512]{2,1,0:T(8,128)(2,1)} %get-tuple-element.13), channel_id=1, source_target_pairs={{0,14},{1,15},{2,4},{3,5},{4,2},{5,3},{6,8},{7,9},{8,6},{9,7},{10,... | collective-permute-start | bytes 1572872 | tf_op jit(solution)/shard_map/ppermute | solution.py:31
  54.3 0.0 collective-permute-done.8
  54.4 3.8 %collective-permute-start.9 = (f32[32,128]{1,0:T(8,128)S(1)}, f32[32,128]{1,0:T(8,128)S(1)}, u32[]{:S(2)}, u32[]{:S(2)}) collective-permute-start(f32[32,128]{1,0:T(8,128)S(1)} %add.98), channel_id=1, source_target_pairs={{0,64},{1,65},{2,66},{3,67},{4,68},{5,69},{6,70},{7,71},{8,72},{9,... | collective-permute-start | bytes 49160 | tf_op jit(solution)/shard_map/ppermute | solution.py:31
  58.2 0.0 collective-permute-done
  58.3 6.1 %collective-permute-start.1 = (bf16[2,16,32,128]{3,2,1,0:T(8,128)(2,1)S(1)}, bf16[2,16,32,128]{3,2,1,0:T(8,128)(2,1)S(1)}, u32[]{:S(2)}, u32[]{:S(2)}) collective-permute-start(bf16[2,16,32,128]{3,2,1,0:T(8,128)(2,1)S(1)} %pad_maximum_fusion.1), channel_id=1, source_target_pairs={{0,256},{1,257},{2,258},{3,259},{4,260},{5,261},{6,262},{7,263},{8... | collective-permute-start | bytes 786440 | tf_op jit(solution)/shard_map/ppermute | solution.py:31
  64.4 0.8 constant_dynamic-slice_fusion.3
  65.2 0.0 collective-permute-done.9
  65.2 4.3 %collective-permute-start.10 = (f32[32,128]{1,0:T(8,128)S(1)}, f32[32,128]{1,0:T(8,128)S(1)}, u32[]{:S(2)}, u32[]{:S(2)}) collective-permute-start(f32[32,128]{1,0:T(8,128)S(1)} %add.99), channel_id=1, source_target_pairs={{0,128},{1,129},{2,130},{3,131},{4,132},{5,133},{6,134},{7,135},{8... | collective-permute-start | bytes 49160 | tf_op jit(solution)/shard_map/ppermute | solution.py:31
  69.5 4.4 %collective-permute-done.10 = f32[32,128]{1,0:T(8,128)S(1)} collective-permute-done((f32[32,128]{1,0:T(8,128)S(1)}, f32[32,128]{1,0:T(8,128)S(1)}, u32[]{:S(2)}, u32[]{:S(2)}) %collective-permute-start.10) | collective-permute-done | bytes 16416 | tf_op jit(solution)/shard_map/ppermute | solution.py:31
  74.0 1.9 %collective-permute-start.11 = (f32[32,128]{1,0:T(8,128)S(1)}, f32[32,128]{1,0:T(8,128)S(1)}, u32[]{:S(2)}, u32[]{:S(2)}) collective-permute-start(f32[32,128]{1,0:T(8,128)S(1)} %add.100), channel_id=1, source_target_pairs={{0,256},{1,257},{2,258},{3,259},{4,260},{5,261},{6,262},{7,263},{8... | collective-permute-start | bytes 49160 | tf_op jit(solution)/shard_map/ppermute | solution.py:31
  75.9 0.1 copy.19
  76.7 3.7 %collective-permute-done.11 = f32[32,128]{1,0:T(8,128)S(1)} collective-permute-done((f32[32,128]{1,0:T(8,128)S(1)}, f32[32,128]{1,0:T(8,128)S(1)}, u32[]{:S(2)}, u32[]{:S(2)}) %collective-permute-start.11) | collective-permute-done | bytes 16416 | tf_op jit(solution)/shard_map/ppermute | solution.py:31
  80.5 2.2 %collective-permute-start.12 = (f32[32,128]{1,0:T(8,128)S(1)}, f32[32,128]{1,0:T(8,128)S(1)}, u32[]{:S(2)}, u32[]{:S(2)}) collective-permute-start(f32[32,128]{1,0:T(8,128)S(1)} %add.101), channel_id=1, source_target_pairs={{0,512},{1,513},{2,514},{3,515},{4,516},{5,517},{6,518},{7,519},{8... | collective-permute-start | bytes 49160 | tf_op jit(solution)/shard_map/ppermute | solution.py:31
  82.7 0.0 collective-permute-done.1
  82.8 1.9 %collective-permute-start.3 = (bf16[4,16,32,128]{3,2,1,0:T(8,128)(2,1)S(1)}, bf16[4,16,32,128]{3,2,1,0:T(8,128)(2,1)S(1)}, u32[]{:S(2)}, u32[]{:S(2)}) collective-permute-start(bf16[4,16,32,128]{3,2,1,0:T(8,128)(2,1)S(1)} %pad_maximum_fusion.near_ref), channel_id=1, source_target_pairs={{0,128},{1,129},{2,130},{3,131},{4,132},{5,133},{6,134},{7,135},{8... | collective-permute-start | bytes 1572872 | tf_op jit(solution)/shard_map/ppermute | solution.py:31
  84.7 5.5 %collective-permute-done.12 = f32[32,128]{1,0:T(8,128)S(1)} collective-permute-done((f32[32,128]{1,0:T(8,128)S(1)}, f32[32,128]{1,0:T(8,128)S(1)}, u32[]{:S(2)}, u32[]{:S(2)}) %collective-permute-start.12) | collective-permute-done | bytes 16416 | tf_op jit(solution)/shard_map/ppermute | solution.py:31
  90.2 1.9 %collective-permute-start.13 = (f32[32,128]{1,0:T(8,128)S(1)}, f32[32,128]{1,0:T(8,128)S(1)}, u32[]{:S(2)}, u32[]{:S(2)}) collective-permute-start(f32[32,128]{1,0:T(8,128)S(1)} %get-tuple-element.27), channel_id=1, source_target_pairs={{0,16},{1,17},{2,18},{3,19},{4,20},{5,21},{6,22},{7,23},{8,24},{9,... | collective-permute-start | bytes 49160 | tf_op jit(solution)/shard_map/ppermute | solution.py:31
  92.1 0.5 constant_dynamic-slice_fusion.1
  92.6 0.5 constant_dynamic-slice_fusion
  93.2 0.0 collective-permute-done.5.a_ref
  93.2 0.0 collective-permute-done.6.b_ref
  93.2 1.2 shard_map.139
  94.4 4.9 %all-to-all-start.1 = ((bf16[8,128,512]{2,1,0:T(8,128)(2,1)}), bf16[8,128,512]{2,1,0:T(8,128)(2,1)}, u32[]{:S(2)}, u32[]{:S(2)}) async-start(bf16[8,128,512]{2,1,0:T(8,128)(2,1)} %shard_map.139), calls=%async_computation.1 | async-start | bytes 2097152 | tf_op jit(solution)/shard_map/all_to_all | solution.py:201
  99.3 0.0 collective-permute-done.13
  99.4 2.1 %collective-permute-start.2 = (bf16[4,16,32,128]{3,2,1,0:T(8,128)(2,1)S(1)}, bf16[4,16,32,128]{3,2,1,0:T(8,128)(2,1)S(1)}, u32[]{:S(2)}, u32[]{:S(2)}) collective-permute-start(bf16[4,16,32,128]{3,2,1,0:T(8,128)(2,1)S(1)} %pad_maximum_fusion.near_ref), channel_id=1, source_target_pairs={{0,16},{1,17},{2,18},{3,19},{4,20},{5,21},{6,22},{7,23},{8,24},{9,... | collective-permute-start | bytes 1572872 | tf_op jit(solution)/shard_map/ppermute | solution.py:31
  101.5 2.2 %collective-permute-start.4 = (bf16[4,16,32,128]{3,2,1,0:T(8,128)(2,1)S(1)}, bf16[4,16,32,128]{3,2,1,0:T(8,128)(2,1)S(1)}, u32[]{:S(2)}, u32[]{:S(2)}) collective-permute-start(bf16[4,16,32,128]{3,2,1,0:T(8,128)(2,1)S(1)} %collective-permute-done.3.far_ref), channel_id=1, source_target_pairs={{0,16},{1,17},{2,18},{3,19},{4,20},{5,21},{6,22},{7,23},{8,24},{9,... | collective-permute-start | bytes 1572872 | tf_op jit(solution)/shard_map/ppermute | solution.py:31
  103.7 1.6 %fusion.3 = bf16[1,1,8192]{2,1,0:T(2,128)(2,1)} fusion(f32[1,1,8192]{2,1,0:T(1,128)S(1)} %bitcast.36, bf16[1,32,1,8192]{3,1,2,0:T(8,128)(2,1)} %param.15, s32[]{:T(128)S(6)} %select_n.107, f32[]{:T(128)S(6)} %sub.33), kind=kLoop, calls=%fused_computation.14 | loop fusion | flops 32768 | bytes 65544 | tf_op jit(solution)/shard_map/convert_element_type | solution.py:233
  105.3 2.7 %shard_map.137.first_ref = f32[128,128]{1,0:T(8,128)} custom-call(bf16[128,8192]{1,0:T(8,128)(2,1)} %tok_ref.5, bf16[4,16,32,128]{3,2,1,0:T(8,128)(2,1)S(1)} %pad_maximum_fusion.near_ref, bf16[4,16,32,128]{3,2,1,0:T(8,128)(2,1)S(1)} %collective-permute-done.3.far_ref), custom_call_target="tpu_custom_call" | custom-call | tf_op jit(solution)/shard_map/pallas_call | solution.py:236
  108.0 0.0 collective-permute-done.2.near_ref
  108.0 0.0 collective-permute-done.4.far_ref
  108.0 0.8 copy-done.1
  108.8 2.7 %shard_map.138 = bf16[128,128]{1,0:T(8,128)(2,1)} custom-call(bf16[128,8192]{1,0:T(8,128)(2,1)} %tok_ref.5, bf16[4,16,32,128]{3,2,1,0:T(8,128)(2,1)S(1)} %collective-permute-done.2.near_ref, bf16[4,16,32,128]{3,2,1,0:T(8,128)(2,1)S(1)} %collective-permute-done.4.far_ref, f32[128,128]{1,0:T(8,128)S(1)} %copy-done.2, f32[128,128]{1,0:T(8,128)S(1)} %copy-done.1), custom_call_target="tpu_custom_call" | custom-call | tf_op jit(solution)/shard_map/pallas_call | solution.py:242
  111.5 21.8 %all-to-all-done.1 = bf16[8,128,512]{2,1,0:T(8,128)(2,1)} async-done(((bf16[8,128,512]{2,1,0:T(8,128)(2,1)}), bf16[8,128,512]{2,1,0:T(8,128)(2,1)}, u32[]{:S(2)}, u32[]{:S(2)}) %all-to-all-start.1) | async-done | bytes 1048608 | tf_op jit(solution)/shard_map/all_to_all | solution.py:201
  133.3 1.4 %convert_reduce_fusion = f32[128,512]{1,0:T(8,128)S(1)} fusion(bf16[8,128,512]{2,1,0:T(8,128)(2,1)} %all-to-all-done.1), kind=kLoop, calls=%fused_computation | loop fusion | flops 983040 | bytes 1310720 | tf_op jit(solution)/shard_map/reduce_sum | solution.py:246
  134.7 0.6 fusion.1
  135.3 0.8 copy.22
  (27 shorter events, 0.3 us)
Async XLA Ops:
  1.5 74.4 %copy-start.3 = (bf16[512,128]{1,0:T(8,128)(2,1)S(1)}, bf16[512,128]{1,0:T(8,128)(2,1)}, u32[]{:S(2)}) copy-start(bf16[512,128]{1,0:T(8,128)(2,1)} %param.11) | copy-start | bytes 393220
  3.0 73.1 %copy-start.4 = (bf16[512]{0:T(512)(128)(2,1)S(1)}, bf16[512]{0:T(512)(128)(2,1)}, u32[]{:S(2)}) copy-start(bf16[512]{0:T(512)(128)(2,1)} %param.10) | copy-start | bytes 3076
  3.0 24.5 %all-to-all-start = ((bf16[16,32,128]{2,1,0:T(8,128)(2,1)}), bf16[16,32,128]{2,1,0:T(8,128)(2,1)S(1)}, u32[]{:S(2)}, u32[]{:S(2)}) async-start(bf16[16,32,128]{2,1,0:T(8,128)(2,1)} %broadcast_in_dim.8), calls=%async_computation | async-start | bytes 262144 | tf_op jit(solution)/shard_map/all_to_all | solution.py:184
  15.7 26.4 %collective-permute-start.7 = (bf16[32,128]{1,0:T(8,128)(2,1)S(1)}, bf16[32,128]{1,0:T(8,128)(2,1)S(1)}, u32[]{:S(2)}, u32[]{:S(2)}) collective-permute-start(bf16[32,128]{1,0:T(8,128)(2,1)S(1)} %bitcast.44), channel_id=1, source_target_pairs={{0,16},{1,17},{2,18},{3,19},{4,20},{5,21},{6,22},{7,23},{8,24},{9,... | collective-permute-start | bytes 24584 | tf_op jit(solution)/shard_map/ppermute | solution.py:31
  27.5 30.7 %collective-permute-start = (bf16[1,16,32,128]{3,2,1,0:T(8,128)(2,1)S(1)}, bf16[1,16,32,128]{3,2,1,0:T(8,128)(2,1)S(1)}, u32[]{:S(2)}, u32[]{:S(2)}) collective-permute-start(bf16[1,16,32,128]{3,2,1,0:T(8,128)(2,1)S(1)} %bitcast.34), channel_id=1, source_target_pairs={{0,512},{1,513},{2,514},{3,515},{4,516},{5,517},{6,518},{7,519},{8... | collective-permute-start | bytes 393224 | tf_op jit(solution)/shard_map/ppermute | solution.py:31
  42.0 12.3 %collective-permute-start.8 = (f32[32,128]{1,0:T(8,128)S(1)}, f32[32,128]{1,0:T(8,128)S(1)}, u32[]{:S(2)}, u32[]{:S(2)}) collective-permute-start(f32[32,128]{1,0:T(8,128)S(1)} %convert_add_fusion), channel_id=1, source_target_pairs={{0,32},{1,33},{2,34},{3,35},{4,36},{5,37},{6,38},{7,39},{8,40},{9,... | collective-permute-start | bytes 49160 | tf_op jit(solution)/shard_map/ppermute | solution.py:31
  49.1 44.1 %copy-start = (bf16[8,128,512]{2,1,0:T(8,128)(2,1)S(1)}, bf16[8,128,512]{2,1,0:T(8,128)(2,1)}, u32[]{:S(2)}) copy-start(bf16[8,128,512]{2,1,0:T(8,128)(2,1)} %get-tuple-element.11.keep_ref) | copy-start | bytes 3145732
  49.1 44.1 %collective-permute-start.5 = (bf16[4,128,512]{2,1,0:T(8,128)(2,1)}, bf16[4,128,512]{2,1,0:T(8,128)(2,1)S(1)}, u32[]{:S(2)}, u32[]{:S(2)}) collective-permute-start(bf16[4,128,512]{2,1,0:T(8,128)(2,1)} %get-tuple-element.12), channel_id=1, source_target_pairs={{0,2},{1,3},{2,0},{3,1},{4,6},{5,7},{6,4},{7,5},{8,10},{9,11},{10,... | collective-permute-start | bytes 1572872 | tf_op jit(solution)/shard_map/ppermute | solution.py:31
  51.5 41.7 %collective-permute-start.6 = (bf16[4,128,512]{2,1,0:T(8,128)(2,1)}, bf16[4,128,512]{2,1,0:T(8,128)(2,1)S(1)}, u32[]{:S(2)}, u32[]{:S(2)}) collective-permute-start(bf16[4,128,512]{2,1,0:T(8,128)(2,1)} %get-tuple-element.13), channel_id=1, source_target_pairs={{0,14},{1,15},{2,4},{3,5},{4,2},{5,3},{6,8},{7,9},{8,6},{9,7},{10,... | collective-permute-start | bytes 1572872 | tf_op jit(solution)/shard_map/ppermute | solution.py:31
  54.4 10.8 %collective-permute-start.9 = (f32[32,128]{1,0:T(8,128)S(1)}, f32[32,128]{1,0:T(8,128)S(1)}, u32[]{:S(2)}, u32[]{:S(2)}) collective-permute-start(f32[32,128]{1,0:T(8,128)S(1)} %add.98), channel_id=1, source_target_pairs={{0,64},{1,65},{2,66},{3,67},{4,68},{5,69},{6,70},{7,71},{8,72},{9,... | collective-permute-start | bytes 49160 | tf_op jit(solution)/shard_map/ppermute | solution.py:31
  58.3 24.4 %collective-permute-start.1 = (bf16[2,16,32,128]{3,2,1,0:T(8,128)(2,1)S(1)}, bf16[2,16,32,128]{3,2,1,0:T(8,128)(2,1)S(1)}, u32[]{:S(2)}, u32[]{:S(2)}) collective-permute-start(bf16[2,16,32,128]{3,2,1,0:T(8,128)(2,1)S(1)} %pad_maximum_fusion.1), channel_id=1, source_target_pairs={{0,256},{1,257},{2,258},{3,259},{4,260},{5,261},{6,262},{7,263},{8... | collective-permute-start | bytes 786440 | tf_op jit(solution)/shard_map/ppermute | solution.py:31
  65.2 8.8 %collective-permute-start.10 = (f32[32,128]{1,0:T(8,128)S(1)}, f32[32,128]{1,0:T(8,128)S(1)}, u32[]{:S(2)}, u32[]{:S(2)}) collective-permute-start(f32[32,128]{1,0:T(8,128)S(1)} %add.99), channel_id=1, source_target_pairs={{0,128},{1,129},{2,130},{3,131},{4,132},{5,133},{6,134},{7,135},{8... | collective-permute-start | bytes 49160 | tf_op jit(solution)/shard_map/ppermute | solution.py:31
  74.0 6.5 %collective-permute-start.11 = (f32[32,128]{1,0:T(8,128)S(1)}, f32[32,128]{1,0:T(8,128)S(1)}, u32[]{:S(2)}, u32[]{:S(2)}) collective-permute-start(f32[32,128]{1,0:T(8,128)S(1)} %add.100), channel_id=1, source_target_pairs={{0,256},{1,257},{2,258},{3,259},{4,260},{5,261},{6,262},{7,263},{8... | collective-permute-start | bytes 49160 | tf_op jit(solution)/shard_map/ppermute | solution.py:31
  80.5 9.7 %collective-permute-start.12 = (f32[32,128]{1,0:T(8,128)S(1)}, f32[32,128]{1,0:T(8,128)S(1)}, u32[]{:S(2)}, u32[]{:S(2)}) collective-permute-start(f32[32,128]{1,0:T(8,128)S(1)} %add.101), channel_id=1, source_target_pairs={{0,512},{1,513},{2,514},{3,515},{4,516},{5,517},{6,518},{7,519},{8... | collective-permute-start | bytes 49160 | tf_op jit(solution)/shard_map/ppermute | solution.py:31
  82.8 18.7 %collective-permute-start.3 = (bf16[4,16,32,128]{3,2,1,0:T(8,128)(2,1)S(1)}, bf16[4,16,32,128]{3,2,1,0:T(8,128)(2,1)S(1)}, u32[]{:S(2)}, u32[]{:S(2)}) collective-permute-start(bf16[4,16,32,128]{3,2,1,0:T(8,128)(2,1)S(1)} %pad_maximum_fusion.near_ref), channel_id=1, source_target_pairs={{0,128},{1,129},{2,130},{3,131},{4,132},{5,133},{6,134},{7,135},{8... | collective-permute-start | bytes 1572872 | tf_op jit(solution)/shard_map/ppermute | solution.py:31
  90.2 9.1 %collective-permute-start.13 = (f32[32,128]{1,0:T(8,128)S(1)}, f32[32,128]{1,0:T(8,128)S(1)}, u32[]{:S(2)}, u32[]{:S(2)}) collective-permute-start(f32[32,128]{1,0:T(8,128)S(1)} %get-tuple-element.27), channel_id=1, source_target_pairs={{0,16},{1,17},{2,18},{3,19},{4,20},{5,21},{6,22},{7,23},{8,24},{9,... | collective-permute-start | bytes 49160 | tf_op jit(solution)/shard_map/ppermute | solution.py:31
  94.4 38.9 %all-to-all-start.1 = ((bf16[8,128,512]{2,1,0:T(8,128)(2,1)}), bf16[8,128,512]{2,1,0:T(8,128)(2,1)}, u32[]{:S(2)}, u32[]{:S(2)}) async-start(bf16[8,128,512]{2,1,0:T(8,128)(2,1)} %shard_map.139), calls=%async_computation.1 | async-start | bytes 2097152 | tf_op jit(solution)/shard_map/all_to_all | solution.py:201
  99.3 8.7 %copy-start.2 = (f32[128,128]{1,0:T(8,128)S(1)}, f32[128,128]{1,0:T(8,128)}, u32[]{:S(2)}) copy-start(f32[128,128]{1,0:T(8,128)} %get-tuple-element.10.inv_ref) | copy-start | bytes 196612
  99.4 8.6 %collective-permute-start.2 = (bf16[4,16,32,128]{3,2,1,0:T(8,128)(2,1)S(1)}, bf16[4,16,32,128]{3,2,1,0:T(8,128)(2,1)S(1)}, u32[]{:S(2)}, u32[]{:S(2)}) collective-permute-start(bf16[4,16,32,128]{3,2,1,0:T(8,128)(2,1)S(1)} %pad_maximum_fusion.near_ref), channel_id=1, source_target_pairs={{0,16},{1,17},{2,18},{3,19},{4,20},{5,21},{6,22},{7,23},{8,24},{9,... | collective-permute-start | bytes 1572872 | tf_op jit(solution)/shard_map/ppermute | solution.py:31
  101.5 6.5 %collective-permute-start.4 = (bf16[4,16,32,128]{3,2,1,0:T(8,128)(2,1)S(1)}, bf16[4,16,32,128]{3,2,1,0:T(8,128)(2,1)S(1)}, u32[]{:S(2)}, u32[]{:S(2)}) collective-permute-start(bf16[4,16,32,128]{3,2,1,0:T(8,128)(2,1)S(1)} %collective-permute-done.3.far_ref), channel_id=1, source_target_pairs={{0,16},{1,17},{2,18},{3,19},{4,20},{5,21},{6,22},{7,23},{8,24},{9,... | collective-permute-start | bytes 1572872 | tf_op jit(solution)/shard_map/ppermute | solution.py:31
  108.0 0.8 copy-start.1

commit v3 on v2

--- a/solution.py
+++ b/solution.py
@@ -43,14 +43,6 @@
     return z, y, c, other_pair(x, 8)
 
 
-def y_one(z, y, c, x):
-    return z, y ^ 1, c, x
-
-
-def y_two(z, y, c, x):
-    return z, y ^ 2, c, x
-
-
 def z_one(z, y, c, x):
     return z ^ 1, y, c, x
 
@@ -95,12 +87,12 @@
 
 def factor_parts(tokens, cot, chunk):
     hd = cot.shape[1]
-    half = jax.ShapeDtypeStruct((4, hd, chunk), jnp.bfloat16)
+    half = pltpu.VMEM((4, hd, chunk), jnp.bfloat16)
     return pl.pallas_call(
         factor_kernel,
         out_shape=(
-            jax.ShapeDtypeStruct((tokens.shape[0], 128), jnp.float32),
-            jax.ShapeDtypeStruct((8, hd, chunk), jnp.bfloat16),
+            pltpu.VMEM((tokens.shape[0], 128), jnp.float32),
+            pltpu.VMEM((8, hd, chunk), jnp.bfloat16),
             half,
             half,
         ),
@@ -209,12 +201,11 @@
         return lax.dynamic_index_in_dim(values, core, 1, keepdims=False)
 
     inner_row = row_of(inner_params[0])
-    other_core = permute(
-        lax.dynamic_index_in_dim(inner_row, 1 - core, 1, keepdims=False), core_swap
-    )
-    total = half_of(inner_row).astype(jnp.float32) + other_core.astype(jnp.float32)
-    for move in (y_one, y_two, z_one, z_two, z_four):
-        total = total + permute(total, move)
+    halves = jnp.broadcast_to(
+        inner_row.transpose(1, 0, 2)[None], (replicas // 2, 2, blocks[0], blocks[2])
+    ).reshape(replicas, blocks[0], blocks[2])
+    inner_all = lax.all_to_all(halves, "replica", 0, 0)
+    total = jnp.sum(inner_all.astype(jnp.float32), axis=0)
     outer_now = half_of(row_of(outer_params))
     momentum_now = half_of(row_of(outer_momentum))
     pseudo_grad = outer_now - total / replicas
@@ -235,7 +226,7 @@
     out = jax.ShapeDtypeStruct((tokens.shape[0], hd), jnp.bfloat16)
     first = pl.pallas_call(
         keys_first,
-        out_shape=jax.ShapeDtypeStruct(out.shape, jnp.float32),
+        out_shape=pltpu.VMEM(out.shape, jnp.float32),
         in_specs=[VMEM] * 3,
         out_specs=VMEM,
     )(tokens, *on_chip(w_near, w_far))

time: 137 us -> 129 us (0.942)
  the two profiles are of different devices: /device:TPU:32 before, /device:TPU:1 now
where the time goes in v3:
time: 129 us; the launch traced here: 128 us
  starting transfers between devices  48.6 us (38%)
  waiting for transfers between devices  26.7 us (21%)
  blocking collectives  25.3 us (20%)
  other arithmetic  9.65 us (7%)
  Pallas kernels  9.02 us (7%)
  local copies, waits for them, and re-layouts  6.41 us (5%)
  between operations  2.28 us (2%)
    ppermute x8, starting transfers between devices, permute(): return lax.ppermute(value, ALL, route(move))  33.1 us
    all_to_all x1, blocking collectives, step(): lax.all_to_all(jnp.broadcast_to(scaled_piece[None], (shards, piece, hd)),...  25.3 us
    all_to_all x1, waiting for transfers between devices, step(): mine = lax.all_to_all(part, 'fsdp', 0, 0, axis_index_groups=x_groups)  16.5 us
    all_to_all x1, starting transfers between devices, step(): inner_all = lax.all_to_all(halves, 'replica', 0, 0)  11.2 us
    ppermute x8, waiting for transfers between devices, permute(): return lax.ppermute(value, ALL, route(move))  10.2 us
    all_to_all x1, starting transfers between devices, step(): mine = lax.all_to_all(part, 'fsdp', 0, 0, axis_index_groups=x_groups)  4.26 us
    pallas_call x1, Pallas kernels, factor_parts(): pl.pallas_call(factor_kernel, out_shape=(pltpu.VMEM((tokens.shape[0], 128...  3.05 us
    pallas_call x1, Pallas kernels, step(): pl.pallas_call(keys_second, out_shape=out, in_specs=[VMEM] * 5, out_specs...  2.71 us
  transfers between devices with their start and end apart: 10, of which 6 were waited for; matrix products, arithmetic and copies ran while one was open for 9% of the time, Pallas kernels for 7%

profile of v3, /device:TPU:1, one launch (start us, length us, event | category | flops | bytes accessed | tf_op | source)
XLA Modules:
  0.0 128.0 jit_solution(11547750760414410939)
XLA Ops:
  0.7 0.8 dynamic-slice_convert_fusion
  1.5 0.8 multiply_convert_fusion
  2.3 25.3 %all_to_all.15 = bf16[16,32,128]{2,1,0:T(8,128)(2,1)S(1)} all-to-all(bf16[16,32,128]{2,1,0:T(8,128)(2,1)S(1)} %broadcast_in_dim.10), channel_id=1, replica_groups=mesh['replica'=64,'fsdp'=16] {'fsdp'}, dimensions={0} | all-to-all | bytes 262144 | tf_op jit(solution)/shard_map/all_to_all | solution.py:176
  27.6 14.3 %collective-permute-start = (bf16[1,16,32,128]{3,2,1,0:T(8,128)(2,1)S(1)}, bf16[1,16,32,128]{3,2,1,0:T(8,128)(2,1)}, u32[]{:S(2)}, u32[]{:S(2)}) collective-permute-start(bf16[1,16,32,128]{3,2,1,0:T(8,128)(2,1)S(1)} %bitcast.38), channel_id=1, source_target_pairs={{0,512},{1,513},{2,514},{3,515},{4,516},{5,517},{6,518},{7,519},{8... | collective-permute-start | bytes 393224 | tf_op jit(solution)/shard_map/ppermute | solution.py:31
  42.5 1.0 dynamic-slice_reduce_fusion
  43.5 1.0 broadcast_in_dim.27
  44.5 11.2 %all-to-all-start.2 = ((bf16[64,32,128]{2,1,0:T(8,128)(2,1)}), bf16[64,32,128]{2,1,0:T(8,128)(2,1)}, u32[]{:S(2)}, u32[]{:S(2)}) async-start(bf16[64,32,128]{2,1,0:T(8,128)(2,1)} %bitcast.7), calls=%async_computation.2 | async-start | bytes 1048576 | tf_op jit(solution)/shard_map/all_to_all | solution.py:207
  55.7 3.1 %shard_map.136 = (f32[128,128]{1,0:T(8,128)S(1)}, bf16[8,128,512]{2,1,0:T(8,128)(2,1)S(1)}, bf16[4,128,512]{2,1,0:T(8,128)(2,1)S(1)}, bf16[4,128,512]{2,1,0:T(8,128)(2,1)S(1)}) custom-call(bf16[128,8192]{1,0:T(8,128)(2,1)} %tok_ref.5, bf16[128,128]{1,0:T(8,128)(2,1)} %cot_ref.1), custom_call_target="tpu_custom_call" | custom-call | tf_op jit(solution)/shard_map/pallas_call | solution.py:91
  58.8 2.0 %collective-permute-start.5 = (bf16[4,128,512]{2,1,0:T(8,128)(2,1)S(1)}, bf16[4,128,512]{2,1,0:T(8,128)(2,1)S(1)}, u32[]{:S(2)}, u32[]{:S(2)}) collective-permute-start(bf16[4,128,512]{2,1,0:T(8,128)(2,1)S(1)} %get-tuple-element.12), channel_id=1, source_target_pairs={{0,2},{1,3},{2,0},{3,1},{4,6},{5,7},{6,4},{7,5},{8,10},{9,11},{10,... | collective-permute-start | bytes 1572872 | tf_op jit(solution)/shard_map/ppermute | solution.py:31
  60.8 2.5 %collective-permute-start.6 = (bf16[4,128,512]{2,1,0:T(8,128)(2,1)S(1)}, bf16[4,128,512]{2,1,0:T(8,128)(2,1)S(1)}, u32[]{:S(2)}, u32[]{:S(2)}) collective-permute-start(bf16[4,128,512]{2,1,0:T(8,128)(2,1)S(1)} %get-tuple-element.13), channel_id=1, source_target_pairs={{0,14},{1,15},{2,4},{3,5},{4,2},{5,3},{6,8},{7,9},{8,6},{9,7},{10,... | collective-permute-start | bytes 1572872 | tf_op jit(solution)/shard_map/ppermute | solution.py:31
  63.4 0.0 copy-done.1
  63.4 0.0 collective-permute-done
  63.4 1.0 broadcast_select_fusion.3
  64.4 0.7 pad_maximum_fusion.1
  65.1 4.2 %collective-permute-start.1 = (bf16[2,16,32,128]{3,2,1,0:T(8,128)(2,1)}, bf16[2,16,32,128]{3,2,1,0:T(8,128)(2,1)}, u32[]{:S(2)}, u32[]{:S(2)}) collective-permute-start(bf16[2,16,32,128]{3,2,1,0:T(8,128)(2,1)} %pad_maximum_fusion.1), channel_id=1, source_target_pairs={{0,256},{1,257},{2,258},{3,259},{4,260},{5,261},{6,262},{7,263},{8... | collective-permute-start | bytes 786440 | tf_op jit(solution)/shard_map/ppermute | solution.py:31
  69.3 0.8 constant_dynamic-slice_fusion.3
  70.1 1.7 %copy.31 = bf16[512,128]{0,1:T(8,128)(2,1)} copy(bf16[512,128]{1,0:T(8,128)(2,1)} %param.11) | data formatting | bytes 262144 | tf_op args[2]
  71.7 0.0 copy-done.3
  71.7 0.6 convert_element_type.49
  73.0 0.7 collective-permute-done.5.a_ref
  73.7 2.9 %collective-permute-done.6.b_ref = bf16[4,128,512]{2,1,0:T(8,128)(2,1)S(1)} collective-permute-done((bf16[4,128,512]{2,1,0:T(8,128)(2,1)S(1)}, bf16[4,128,512]{2,1,0:T(8,128)(2,1)S(1)}, u32[]{:S(2)}, u32[]{:S(2)}) %collective-permute-start.6) | collective-permute-done | bytes 524320 | tf_op jit(solution)/shard_map/ppermute | solution.py:31
  76.6 1.2 shard_map.139
  77.8 5.2 %collective-permute-done.1 = bf16[2,16,32,128]{3,2,1,0:T(8,128)(2,1)} collective-permute-done((bf16[2,16,32,128]{3,2,1,0:T(8,128)(2,1)}, bf16[2,16,32,128]{3,2,1,0:T(8,128)(2,1)}, u32[]{:S(2)}, u32[]{:S(2)}) %collective-permute-start.1) | collective-permute-done | bytes 262176 | tf_op jit(solution)/shard_map/ppermute | solution.py:31
  83.0 1.0 broadcast_select_fusion.1
  84.0 1.9 %collective-permute-start.3 = (bf16[4,16,32,128]{3,2,1,0:T(8,128)(2,1)S(1)}, bf16[4,16,32,128]{3,2,1,0:T(8,128)(2,1)S(1)}, u32[]{:S(2)}, u32[]{:S(2)}) collective-permute-start(bf16[4,16,32,128]{3,2,1,0:T(8,128)(2,1)S(1)} %pad_maximum_fusion.near_ref), channel_id=1, source_target_pairs={{0,128},{1,129},{2,130},{3,131},{4,132},{5,133},{6,134},{7,135},{8... | collective-permute-start | bytes 1572872 | tf_op jit(solution)/shard_map/ppermute | solution.py:31
  86.0 2.7 %collective-permute-start.2 = (bf16[4,16,32,128]{3,2,1,0:T(8,128)(2,1)S(1)}, bf16[4,16,32,128]{3,2,1,0:T(8,128)(2,1)S(1)}, u32[]{:S(2)}, u32[]{:S(2)}) collective-permute-start(bf16[4,16,32,128]{3,2,1,0:T(8,128)(2,1)S(1)} %pad_maximum_fusion.near_ref), channel_id=1, source_target_pairs={{0,16},{1,17},{2,18},{3,19},{4,20},{5,21},{6,22},{7,23},{8,24},{9,... | collective-permute-start | bytes 1572872 | tf_op jit(solution)/shard_map/ppermute | solution.py:31
  88.7 0.0 all-to-all-done.2
  88.7 4.3 %all-to-all-start.1 = ((bf16[8,128,512]{2,1,0:T(8,128)(2,1)}), bf16[8,128,512]{2,1,0:T(8,128)(2,1)}, u32[]{:S(2)}, u32[]{:S(2)}) async-start(bf16[8,128,512]{2,1,0:T(8,128)(2,1)} %shard_map.139), calls=%async_computation.1 | async-start | bytes 2097152 | tf_op jit(solution)/shard_map/all_to_all | solution.py:193
  93.0 1.1 convert_reduce_fusion.1
  94.1 1.9 %collective-permute-start.7 = (f32[32,128]{1,0:T(8,128)S(1)}, f32[32,128]{1,0:T(8,128)S(1)}, u32[]{:S(2)}, u32[]{:S(2)}) collective-permute-start(f32[32,128]{1,0:T(8,128)S(1)} %get-tuple-element.39), channel_id=1, source_target_pairs={{0,16},{1,17},{2,18},{3,19},{4,20},{5,21},{6,22},{7,23},{8,24},{9,... | collective-permute-start | bytes 49160 | tf_op jit(solution)/shard_map/ppermute | solution.py:31
  96.0 0.5 constant_dynamic-slice_fusion.1
  96.6 0.5 constant_dynamic-slice_fusion
  97.1 0.1 collective-permute-done.7
  97.2 1.4 %collective-permute-done.3.far_ref = bf16[4,16,32,128]{3,2,1,0:T(8,128)(2,1)S(1)} collective-permute-done((bf16[4,16,32,128]{3,2,1,0:T(8,128)(2,1)S(1)}, bf16[4,16,32,128]{3,2,1,0:T(8,128)(2,1)S(1)}, u32[]{:S(2)}, u32[]{:S(2)}) %collective-permute-start.3) | collective-permute-done | bytes 524320 | tf_op jit(solution)/shard_map/ppermute | solution.py:31
  98.6 3.6 %collective-permute-start.4 = (bf16[4,16,32,128]{3,2,1,0:T(8,128)(2,1)S(1)}, bf16[4,16,32,128]{3,2,1,0:T(8,128)(2,1)S(1)}, u32[]{:S(2)}, u32[]{:S(2)}) collective-permute-start(bf16[4,16,32,128]{3,2,1,0:T(8,128)(2,1)S(1)} %collective-permute-done.3.far_ref), channel_id=1, source_target_pairs={{0,16},{1,17},{2,18},{3,19},{4,20},{5,21},{6,22},{7,23},{8,24},{9,... | collective-permute-start | bytes 1572872 | tf_op jit(solution)/shard_map/ppermute | solution.py:31
  102.2 1.6 %fusion.3 = bf16[1,1,8192]{2,1,0:T(2,128)(2,1)} fusion(f32[1,1,8192]{2,1,0:T(1,128)S(1)} %bitcast.43, bf16[1,32,1,8192]{3,1,2,0:T(8,128)(2,1)} %param.15, s32[]{:T(128)S(6)} %select_n.102, f32[]{:T(128)S(6)} %sub.37), kind=kLoop, calls=%fused_computation.15 | loop fusion | flops 32768 | bytes 65544 | tf_op jit(solution)/shard_map/convert_element_type | solution.py:224
  103.7 2.0 %shard_map.137.first_ref = f32[128,128]{1,0:T(8,128)S(1)} custom-call(bf16[128,8192]{1,0:T(8,128)(2,1)} %tok_ref.5, bf16[4,16,32,128]{3,2,1,0:T(8,128)(2,1)S(1)} %pad_maximum_fusion.near_ref, bf16[4,16,32,128]{3,2,1,0:T(8,128)(2,1)S(1)} %collective-permute-done.3.far_ref), custom_call_target="tpu_custom_call" | custom-call | tf_op jit(solution)/shard_map/pallas_call | solution.py:227
  105.8 0.0 collective-permute-done.2.near_ref
  105.8 0.0 collective-permute-done.4.far_ref
  105.8 0.0 copy-start
  105.8 0.0 copy-start.2
  105.8 2.7 %shard_map.138 = bf16[128,128]{1,0:T(8,128)(2,1)} custom-call(bf16[128,8192]{1,0:T(8,128)(2,1)} %tok_ref.5, bf16[4,16,32,128]{3,2,1,0:T(8,128)(2,1)S(1)} %collective-permute-done.2.near_ref, bf16[4,16,32,128]{3,2,1,0:T(8,128)(2,1)S(1)} %collective-permute-done.4.far_ref, f32[128,128]{1,0:T(8,128)S(1)} %get-tuple-element.10.inv_ref, ...), custom_call_target="tpu_custom_call" | custom-call | tf_op jit(solution)/shard_map/pallas_call | solution.py:233
  108.6 16.5 %all-to-all-done.1 = bf16[8,128,512]{2,1,0:T(8,128)(2,1)} async-done(((bf16[8,128,512]{2,1,0:T(8,128)(2,1)}), bf16[8,128,512]{2,1,0:T(8,128)(2,1)}, u32[]{:S(2)}, u32[]{:S(2)}) %all-to-all-start.1) | async-done | bytes 1048608 | tf_op jit(solution)/shard_map/all_to_all | solution.py:193
  125.1 1.4 %convert_reduce_fusion = f32[128,512]{1,0:T(8,128)S(1)} fusion(bf16[8,128,512]{2,1,0:T(8,128)(2,1)} %all-to-all-done.1), kind=kLoop, calls=%fused_computation | loop fusion | flops 983040 | bytes 1310720 | tf_op jit(solution)/shard_map/reduce_sum | solution.py:237
  126.5 0.0 copy-done
  126.5 0.0 copy-done.2
  126.5 0.6 fusion.1
  127.1 0.8 copy.36
  (11 shorter events, 0.2 us)
Async XLA Ops:
  27.6 35.8 %copy-start.1 = (bf16[16,32,128]{2,1,0:T(8,128)(2,1)}, bf16[16,32,128]{2,1,0:T(8,128)(2,1)S(1)}, u32[]{:S(2)}) copy-start(bf16[16,32,128]{2,1,0:T(8,128)(2,1)S(1)} %all_to_all.15) | copy-start | bytes 393220
  27.6 35.8 %collective-permute-start = (bf16[1,16,32,128]{3,2,1,0:T(8,128)(2,1)S(1)}, bf16[1,16,32,128]{3,2,1,0:T(8,128)(2,1)}, u32[]{:S(2)}, u32[]{:S(2)}) collective-permute-start(bf16[1,16,32,128]{3,2,1,0:T(8,128)(2,1)S(1)} %bitcast.38), channel_id=1, source_target_pairs={{0,512},{1,513},{2,514},{3,515},{4,516},{5,517},{6,518},{7,519},{8... | collective-permute-start | bytes 393224 | tf_op jit(solution)/shard_map/ppermute | solution.py:31
  44.5 27.2 %copy-start.3 = (bf16[512]{0:T(512)(128)(2,1)S(1)}, bf16[512]{0:T(512)(128)(2,1)}, u32[]{:S(2)}) copy-start(bf16[512]{0:T(512)(128)(2,1)} %param.10) | copy-start | bytes 3076
  44.5 44.2 %all-to-all-start.2 = ((bf16[64,32,128]{2,1,0:T(8,128)(2,1)}), bf16[64,32,128]{2,1,0:T(8,128)(2,1)}, u32[]{:S(2)}, u32[]{:S(2)}) async-start(bf16[64,32,128]{2,1,0:T(8,128)(2,1)} %bitcast.7), calls=%async_computation.2 | async-start | bytes 1048576 | tf_op jit(solution)/shard_map/all_to_all | solution.py:207
  58.8 15.0 %collective-permute-start.5 = (bf16[4,128,512]{2,1,0:T(8,128)(2,1)S(1)}, bf16[4,128,512]{2,1,0:T(8,128)(2,1)S(1)}, u32[]{:S(2)}, u32[]{:S(2)}) collective-permute-start(bf16[4,128,512]{2,1,0:T(8,128)(2,1)S(1)} %get-tuple-element.12), channel_id=1, source_target_pairs={{0,2},{1,3},{2,0},{3,1},{4,6},{5,7},{6,4},{7,5},{8,10},{9,11},{10,... | collective-permute-start | bytes 1572872 | tf_op jit(solution)/shard_map/ppermute | solution.py:31
  60.8 15.8 %collective-permute-start.6 = (bf16[4,128,512]{2,1,0:T(8,128)(2,1)S(1)}, bf16[4,128,512]{2,1,0:T(8,128)(2,1)S(1)}, u32[]{:S(2)}, u32[]{:S(2)}) collective-permute-start(bf16[4,128,512]{2,1,0:T(8,128)(2,1)S(1)} %get-tuple-element.13), channel_id=1, source_target_pairs={{0,14},{1,15},{2,4},{3,5},{4,2},{5,3},{6,8},{7,9},{8,6},{9,7},{10,... | collective-permute-start | bytes 1572872 | tf_op jit(solution)/shard_map/ppermute | solution.py:31
  65.1 17.9 %collective-permute-start.1 = (bf16[2,16,32,128]{3,2,1,0:T(8,128)(2,1)}, bf16[2,16,32,128]{3,2,1,0:T(8,128)(2,1)}, u32[]{:S(2)}, u32[]{:S(2)}) collective-permute-start(bf16[2,16,32,128]{3,2,1,0:T(8,128)(2,1)} %pad_maximum_fusion.1), channel_id=1, source_target_pairs={{0,256},{1,257},{2,258},{3,259},{4,260},{5,261},{6,262},{7,263},{8... | collective-permute-start | bytes 786440 | tf_op jit(solution)/shard_map/ppermute | solution.py:31
  84.0 14.6 %collective-permute-start.3 = (bf16[4,16,32,128]{3,2,1,0:T(8,128)(2,1)S(1)}, bf16[4,16,32,128]{3,2,1,0:T(8,128)(2,1)S(1)}, u32[]{:S(2)}, u32[]{:S(2)}) collective-permute-start(bf16[4,16,32,128]{3,2,1,0:T(8,128)(2,1)S(1)} %pad_maximum_fusion.near_ref), channel_id=1, source_target_pairs={{0,128},{1,129},{2,130},{3,131},{4,132},{5,133},{6,134},{7,135},{8... | collective-permute-start | bytes 1572872 | tf_op jit(solution)/shard_map/ppermute | solution.py:31
  86.0 19.9 %collective-permute-start.2 = (bf16[4,16,32,128]{3,2,1,0:T(8,128)(2,1)S(1)}, bf16[4,16,32,128]{3,2,1,0:T(8,128)(2,1)S(1)}, u32[]{:S(2)}, u32[]{:S(2)}) collective-permute-start(bf16[4,16,32,128]{3,2,1,0:T(8,128)(2,1)S(1)} %pad_maximum_fusion.near_ref), channel_id=1, source_target_pairs={{0,16},{1,17},{2,18},{3,19},{4,20},{5,21},{6,22},{7,23},{8,24},{9,... | collective-permute-start | bytes 1572872 | tf_op jit(solution)/shard_map/ppermute | solution.py:31
  88.7 36.4 %all-to-all-start.1 = ((bf16[8,128,512]{2,1,0:T(8,128)(2,1)}), bf16[8,128,512]{2,1,0:T(8,128)(2,1)}, u32[]{:S(2)}, u32[]{:S(2)}) async-start(bf16[8,128,512]{2,1,0:T(8,128)(2,1)} %shard_map.139), calls=%async_computation.1 | async-start | bytes 2097152 | tf_op jit(solution)/shard_map/all_to_all | solution.py:193
  94.1 3.1 %collective-permute-start.7 = (f32[32,128]{1,0:T(8,128)S(1)}, f32[32,128]{1,0:T(8,128)S(1)}, u32[]{:S(2)}, u32[]{:S(2)}) collective-permute-start(f32[32,128]{1,0:T(8,128)S(1)} %get-tuple-element.39), channel_id=1, source_target_pairs={{0,16},{1,17},{2,18},{3,19},{4,20},{5,21},{6,22},{7,23},{8,24},{9,... | collective-permute-start | bytes 49160 | tf_op jit(solution)/shard_map/ppermute | solution.py:31
  98.6 7.2 %collective-permute-start.4 = (bf16[4,16,32,128]{3,2,1,0:T(8,128)(2,1)S(1)}, bf16[4,16,32,128]{3,2,1,0:T(8,128)(2,1)S(1)}, u32[]{:S(2)}, u32[]{:S(2)}) collective-permute-start(bf16[4,16,32,128]{3,2,1,0:T(8,128)(2,1)S(1)} %collective-permute-done.3.far_ref), channel_id=1, source_target_pairs={{0,16},{1,17},{2,18},{3,19},{4,20},{5,21},{6,22},{7,23},{8,24},{9,... | collective-permute-start | bytes 1572872 | tf_op jit(solution)/shard_map/ppermute | solution.py:31
  105.8 20.6 %copy-start = (bf16[512,128]{0,1:T(8,128)(2,1)S(1)}, bf16[512,128]{0,1:T(8,128)(2,1)}, u32[]{:S(2)}) copy-start(bf16[512,128]{0,1:T(8,128)(2,1)} %copy.31) | copy-start | bytes 393220
  105.8 20.6 %copy-start.2 = (f32[512]{0:T(512)S(1)}, f32[512]{0:T(512)}, u32[]{:S(2)}) copy-start(f32[512]{0:T(512)} %convert_element_type.49) | copy-start | bytes 6148

commit v4 on v3

--- a/solution.py
+++ b/solution.py
@@ -31,16 +31,8 @@
     return lax.ppermute(value, ALL, route(move))
 
 
-def other_pair(i, n):
-    return (i + 1) % n if i % 2 else (i - 1) % n
-
-
 def x_near(z, y, c, x):
-    return z, y, c, x ^ 1
-
-
-def x_near_other(z, y, c, x):
-    return z, y, c, other_pair(x, 8)
+    return z, y, c, (x + (1 if (x + c) % 2 == 0 else -1)) % 8
 
 
 def z_one(z, y, c, x):
@@ -59,7 +51,7 @@
     return z, y, 1 - c, x
 
 
-def factor_kernel(tok_ref, cot_ref, inv_ref, keep_ref, send_a, send_b):
+def factor_kernel(tok_ref, cot_ref, inv_ref, keep_ref, send_ref):
     tokens, width = tok_ref.shape
     chunk = keep_ref.shape[2]
 
@@ -81,41 +73,37 @@
         return jnp.dot(scaled, columns, preferred_element_type=jnp.float32).astype(jnp.bfloat16)
 
     for slot in range(8):
-        (send_a, send_b)[slot // 4][slot % 4] = product(slot, 1 - parity)
+        send_ref[slot] = product(slot, 1 - parity)
         keep_ref[slot] = product(slot, parity)
 
 
 def factor_parts(tokens, cot, chunk):
     hd = cot.shape[1]
-    half = pltpu.VMEM((4, hd, chunk), jnp.bfloat16)
     return pl.pallas_call(
         factor_kernel,
         out_shape=(
             pltpu.VMEM((tokens.shape[0], 128), jnp.float32),
             pltpu.VMEM((8, hd, chunk), jnp.bfloat16),
-            half,
-            half,
+            pltpu.VMEM((8, hd, chunk), jnp.bfloat16),
         ),
         in_specs=[VMEM] * 2,
-        out_specs=(VMEM,) * 4,
+        out_specs=(VMEM,) * 3,
     )(tokens, cot)
 
 
-def add_kernel(keep_ref, a_ref, b_ref, out_ref):
+def add_kernel(keep_ref, other_ref, out_ref):
     for slot in range(8):
-        other = (a_ref, b_ref)[slot // 4][slot % 4]
-        out_ref[slot] = (keep_ref[slot].astype(jnp.float32) + other.astype(jnp.float32)).astype(
-            out_ref.dtype
-        )
-
-
-def add_parts(keep, a, b):
+        total = keep_ref[slot].astype(jnp.float32) + other_ref[slot].astype(jnp.float32)
+        out_ref[slot] = total.astype(out_ref.dtype)
+
+
+def add_parts(keep, other):
     return pl.pallas_call(
         add_kernel,
         out_shape=jax.ShapeDtypeStruct(keep.shape, keep.dtype),
-        in_specs=[VMEM] * 3,
+        in_specs=[VMEM] * 2,
         out_specs=VMEM,
-    )(*on_chip(keep, a, b))
+    )(*on_chip(keep, other))
 
 
 def keys_product(tok_ref, w_refs, flip):
@@ -161,9 +149,8 @@
     replicas = lax.axis_size("replica")
     core = replica % 2
 
-    inv, keep, send_a, send_b = factor_parts(tokens, key_cotangent, rows)
-    recv_a = permute(send_a, x_near)
-    recv_b = permute(send_b, x_near_other)
+    inv, keep, send = factor_parts(tokens, key_cotangent, rows)
+    recv = permute(send, x_near)
 
     plane = replica // 8
     piece = rows // 16
@@ -188,7 +175,7 @@
     w_far = permute(w_near, z_one)
     w_near_other = permute(w_near, core_swap)
     w_far_other = permute(w_far, core_swap)
-    part = add_parts(keep, recv_a, recv_b)
+    part = add_parts(keep, recv)
     x_groups = [[4 * k + 2 * p + y for k in range(4) for y in range(2)] for p in range(2)]
     mine = lax.all_to_all(part, "fsdp", 0, 0, axis_index_groups=x_groups)
 

time: 129 us -> 133 us (1.031)
  the two profiles are of different devices: /device:TPU:1 before, /device:TPU:16 now
where the time goes in v4:
time: 133 us
  starting transfers between devices  43.4 us (33%)
  waiting for transfers between devices  39 us (29%)
  blocking collectives  25 us (19%)
  Pallas kernels  11.3 us (8%)
  local copies, waits for them, and re-layouts  6.03 us (5%)
  other arithmetic  5.41 us (4%)
  between operations  2.28 us (2%)
    ppermute x7, starting transfers between devices, permute(): return lax.ppermute(value, ALL, route(move))  29.3 us
    all_to_all x1, blocking collectives, step(): lax.all_to_all(jnp.broadcast_to(scaled_piece[None], (shards, piece, hd)),...  25 us
    all_to_all x1, waiting for transfers between devices, step(): mine = lax.all_to_all(part, 'fsdp', 0, 0, axis_index_groups=x_groups)  24.8 us
    ppermute x7, waiting for transfers between devices, permute(): return lax.ppermute(value, ALL, route(move))  14.2 us
    all_to_all x1, starting transfers between devices, step(): inner_all = lax.all_to_all(halves, 'replica', 0, 0)  9.9 us
    all_to_all x1, starting transfers between devices, step(): mine = lax.all_to_all(part, 'fsdp', 0, 0, axis_index_groups=x_groups)  4.24 us
    pallas_call x1, Pallas kernels, factor_parts(): pl.pallas_call(factor_kernel, out_shape=(pltpu.VMEM((tokens.shape[0], 128...  4.04 us
    pallas_call x1, Pallas kernels, step(): pl.pallas_call(keys_second, out_shape=out, in_specs=[VMEM] * 5, out_specs...  2.68 us
  transfers between devices with their start and end apart: 9, of which 3 were waited for; matrix products, arithmetic and copies ran while one was open for 4% of the time, Pallas kernels for 9%

profile of v4, /device:TPU:16, one launch (start us, length us, event | category | flops | bytes accessed | tf_op | source)
XLA Modules:
  0.0 132.5 jit_solution(4518364860252822145)
XLA Ops:
  0.7 0.8 dynamic-slice_convert_fusion
  1.5 0.8 multiply_convert_fusion
  2.3 25.0 %all_to_all.15 = bf16[16,32,128]{2,1,0:T(8,128)(2,1)S(1)} all-to-all(bf16[16,32,128]{2,1,0:T(8,128)(2,1)S(1)} %broadcast_in_dim.10), channel_id=1, replica_groups=mesh['replica'=64,'fsdp'=16] {'fsdp'}, dimensions={0} | all-to-all | bytes 262144 | tf_op jit(solution)/shard_map/all_to_all | solution.py:163
  27.3 14.5 %collective-permute-start = (bf16[1,16,32,128]{3,2,1,0:T(8,128)(2,1)S(1)}, bf16[1,16,32,128]{3,2,1,0:T(8,128)(2,1)S(1)}, u32[]{:S(2)}, u32[]{:S(2)}) collective-permute-start(bf16[1,16,32,128]{3,2,1,0:T(8,128)(2,1)S(1)} %bitcast.38), channel_id=1, source_target_pairs={{0,512},{1,513},{2,514},{3,515},{4,516},{5,517},{6,518},{7,519},{8... | collective-permute-start | bytes 393224 | tf_op jit(solution)/shard_map/ppermute | solution.py:31
  42.5 1.0 dynamic-slice_reduce_fusion
  43.5 0.9 broadcast_in_dim.27
  44.4 0.0 copy-start.2
  44.4 0.0 copy-start.3
  44.4 9.9 %all-to-all-start.2 = ((bf16[64,32,128]{2,1,0:T(8,128)(2,1)}), bf16[64,32,128]{2,1,0:T(8,128)(2,1)S(1)}, u32[]{:S(2)}, u32[]{:S(2)}) async-start(bf16[64,32,128]{2,1,0:T(8,128)(2,1)} %bitcast.7), calls=%async_computation.2 | async-start | bytes 1048576 | tf_op jit(solution)/shard_map/all_to_all | solution.py:194
  54.3 4.0 %shard_map.136 = (f32[128,128]{1,0:T(8,128)S(1)}, bf16[8,128,512]{2,1,0:T(8,128)(2,1)S(1)}, bf16[8,128,512]{2,1,0:T(8,128)(2,1)}) custom-call(bf16[128,8192]{1,0:T(8,128)(2,1)} %tok_ref.5, bf16[128,128]{1,0:T(8,128)(2,1)} %cot_ref.1), custom_call_target="tpu_custom_call" | custom-call | tf_op jit(solution)/shard_map/pallas_call | solution.py:82
  58.4 0.0 copy-start
  58.4 2.3 %collective-permute-start.5 = (bf16[8,128,512]{2,1,0:T(8,128)(2,1)}, bf16[8,128,512]{2,1,0:T(8,128)(2,1)}, u32[]{:S(2)}, u32[]{:S(2)}) collective-permute-start(bf16[8,128,512]{2,1,0:T(8,128)(2,1)} %get-tuple-element.11), channel_id=1, source_target_pairs={{0,2},{1,3},{2,0},{3,1},{4,6},{5,7},{6,4},{7,5},{8,10},{9,11},{10,... | collective-permute-start | bytes 3145736 | tf_op jit(solution)/shard_map/ppermute | solution.py:31
  60.7 0.0 collective-permute-done
  60.8 4.3 %collective-permute-start.1 = (bf16[2,16,32,128]{3,2,1,0:T(8,128)(2,1)S(1)}, bf16[2,16,32,128]{3,2,1,0:T(8,128)(2,1)S(1)}, u32[]{:S(2)}, u32[]{:S(2)}) collective-permute-start(bf16[2,16,32,128]{3,2,1,0:T(8,128)(2,1)S(1)} %pad_maximum_fusion.1), channel_id=1, source_target_pairs={{0,256},{1,257},{2,258},{3,259},{4,260},{5,261},{6,262},{7,263},{8... | collective-permute-start | bytes 786440 | tf_op jit(solution)/shard_map/ppermute | solution.py:31
  65.0 0.8 constant_dynamic-slice_fusion.3
  65.8 0.0 copy-done.2
  65.8 0.1 copy.31
  66.0 0.0 copy-done.3
  66.7 14.0 %collective-permute-done.1 = bf16[2,16,32,128]{3,2,1,0:T(8,128)(2,1)S(1)} collective-permute-done((bf16[2,16,32,128]{3,2,1,0:T(8,128)(2,1)S(1)}, bf16[2,16,32,128]{3,2,1,0:T(8,128)(2,1)S(1)}, u32[]{:S(2)}, u32[]{:S(2)}) %collective-permute-start.1) | collective-permute-done | bytes 262176 | tf_op jit(solution)/shard_map/ppermute | solution.py:31
  80.8 1.9 %collective-permute-start.3 = (bf16[4,16,32,128]{3,2,1,0:T(8,128)(2,1)S(1)}, bf16[4,16,32,128]{3,2,1,0:T(8,128)(2,1)}, u32[]{:S(2)}, u32[]{:S(2)}) collective-permute-start(bf16[4,16,32,128]{3,2,1,0:T(8,128)(2,1)S(1)} %pad_maximum_fusion.near_ref), channel_id=1, source_target_pairs={{0,128},{1,129},{2,130},{3,131},{4,132},{5,133},{6,134},{7,135},{8... | collective-permute-start | bytes 1572872 | tf_op jit(solution)/shard_map/ppermute | solution.py:31
  82.8 1.9 %collective-permute-start.2 = (bf16[4,16,32,128]{3,2,1,0:T(8,128)(2,1)S(1)}, bf16[4,16,32,128]{3,2,1,0:T(8,128)(2,1)S(1)}, u32[]{:S(2)}, u32[]{:S(2)}) collective-permute-start(bf16[4,16,32,128]{3,2,1,0:T(8,128)(2,1)S(1)} %pad_maximum_fusion.near_ref), channel_id=1, source_target_pairs={{0,16},{1,17},{2,18},{3,19},{4,20},{5,21},{6,22},{7,23},{8,24},{9,... | collective-permute-start | bytes 1572872 | tf_op jit(solution)/shard_map/ppermute | solution.py:31
  84.7 0.0 all-to-all-done.2
  84.7 0.1 convert_reduce_fusion.1
  84.8 0.0 copy-done
  84.8 2.4 %collective-permute-start.6 = (f32[32,128]{1,0:T(8,128)S(1)}, f32[32,128]{1,0:T(8,128)S(1)}, u32[]{:S(2)}, u32[]{:S(2)}) collective-permute-start(f32[32,128]{1,0:T(8,128)S(1)} %get-tuple-element.37), channel_id=1, source_target_pairs={{0,16},{1,17},{2,18},{3,19},{4,20},{5,21},{6,22},{7,23},{8,24},{9,... | collective-permute-start | bytes 49160 | tf_op jit(solution)/shard_map/ppermute | solution.py:31
  87.3 0.5 constant_dynamic-slice_fusion.1
  87.8 0.5 constant_dynamic-slice_fusion
  88.3 0.0 collective-permute-done.5.other_ref
  88.3 0.0 copy-start.1
  88.3 1.2 copy-done.1
  89.5 2.5 %shard_map.139 = bf16[8,128,512]{2,1,0:T(8,128)(2,1)} custom-call(bf16[8,128,512]{2,1,0:T(8,128)(2,1)S(1)} %copy-done.1, bf16[8,128,512]{2,1,0:T(8,128)(2,1)} %collective-permute-done.5.other_ref), custom_call_target="tpu_custom_call" | custom-call | tf_op jit(solution)/shard_map/pallas_call | solution.py:101
  92.0 4.2 %all-to-all-start.1 = ((bf16[8,128,512]{2,1,0:T(8,128)(2,1)}), bf16[8,128,512]{2,1,0:T(8,128)(2,1)}, u32[]{:S(2)}, u32[]{:S(2)}) async-start(bf16[8,128,512]{2,1,0:T(8,128)(2,1)} %shard_map.139), calls=%async_computation.1 | async-start | bytes 2097152 | tf_op jit(solution)/shard_map/all_to_all | solution.py:180
  96.3 0.0 collective-permute-done.6
  96.3 0.2 collective-permute-done.3.far_ref
  96.5 1.9 %collective-permute-start.4 = (bf16[4,16,32,128]{3,2,1,0:T(8,128)(2,1)}, bf16[4,16,32,128]{3,2,1,0:T(8,128)(2,1)S(1)}, u32[]{:S(2)}, u32[]{:S(2)}) collective-permute-start(bf16[4,16,32,128]{3,2,1,0:T(8,128)(2,1)} %collective-permute-done.3.far_ref), channel_id=1, source_target_pairs={{0,16},{1,17},{2,18},{3,19},{4,20},{5,21},{6,22},{7,23},{8,24},{9,... | collective-permute-start | bytes 1572872 | tf_op jit(solution)/shard_map/ppermute | solution.py:31
  98.4 1.6 %fusion.3 = bf16[1,1,8192]{2,1,0:T(2,128)(2,1)} fusion(f32[1,1,8192]{2,1,0:T(1,128)S(1)} %bitcast.43, bf16[1,32,1,8192]{3,1,2,0:T(8,128)(2,1)} %param.15, s32[]{:T(128)S(6)} %select_n.102, f32[]{:T(128)S(6)} %sub.37), kind=kLoop, calls=%fused_computation.15 | loop fusion | flops 32768 | bytes 65544 | tf_op jit(solution)/shard_map/convert_element_type | solution.py:211
  100.0 2.1 %shard_map.137.first_ref = f32[128,128]{1,0:T(8,128)S(1)} custom-call(bf16[128,8192]{1,0:T(8,128)(2,1)} %tok_ref.5, bf16[4,16,32,128]{3,2,1,0:T(8,128)(2,1)S(1)} %pad_maximum_fusion.near_ref, bf16[4,16,32,128]{3,2,1,0:T(8,128)(2,1)} %collective-permute-done.3.far_ref), custom_call_target="tpu_custom_call" | custom-call | tf_op jit(solution)/shard_map/pallas_call | solution.py:214
  102.1 0.0 collective-permute-done.2.near_ref
  102.1 0.0 collective-permute-done.4.far_ref
  102.2 2.7 %shard_map.138 = bf16[128,128]{1,0:T(8,128)(2,1)} custom-call(bf16[128,8192]{1,0:T(8,128)(2,1)} %tok_ref.5, bf16[4,16,32,128]{3,2,1,0:T(8,128)(2,1)S(1)} %collective-permute-done.2.near_ref, bf16[4,16,32,128]{3,2,1,0:T(8,128)(2,1)S(1)} %collective-permute-done.4.far_ref, f32[128,128]{1,0:T(8,128)S(1)} %get-tuple-element.9.inv_ref, ...), custom_call_target="tpu_custom_call" | custom-call | tf_op jit(solution)/shard_map/pallas_call | solution.py:220
  104.8 24.8 %all-to-all-done.1 = bf16[8,128,512]{2,1,0:T(8,128)(2,1)} async-done(((bf16[8,128,512]{2,1,0:T(8,128)(2,1)}), bf16[8,128,512]{2,1,0:T(8,128)(2,1)}, u32[]{:S(2)}, u32[]{:S(2)}) %all-to-all-start.1) | async-done | bytes 1048608 | tf_op jit(solution)/shard_map/all_to_all | solution.py:180
  129.6 1.4 %convert_reduce_fusion = f32[128,512]{1,0:T(8,128)S(1)} fusion(bf16[8,128,512]{2,1,0:T(8,128)(2,1)} %all-to-all-done.1), kind=kLoop, calls=%fused_computation | loop fusion | flops 983040 | bytes 1310720 | tf_op jit(solution)/shard_map/reduce_sum | solution.py:224
  131.0 0.6 fusion.1
  131.7 0.8 copy.36
  (13 shorter events, 0.3 us)
Async XLA Ops:
  27.3 33.4 %collective-permute-start = (bf16[1,16,32,128]{3,2,1,0:T(8,128)(2,1)S(1)}, bf16[1,16,32,128]{3,2,1,0:T(8,128)(2,1)S(1)}, u32[]{:S(2)}, u32[]{:S(2)}) collective-permute-start(bf16[1,16,32,128]{3,2,1,0:T(8,128)(2,1)S(1)} %bitcast.38), channel_id=1, source_target_pairs={{0,512},{1,513},{2,514},{3,515},{4,516},{5,517},{6,518},{7,519},{8... | collective-permute-start | bytes 393224 | tf_op jit(solution)/shard_map/ppermute | solution.py:31
  44.4 21.4 %copy-start.2 = (bf16[512,128]{1,0:T(8,128)(2,1)S(1)}, bf16[512,128]{1,0:T(8,128)(2,1)}, u32[]{:S(2)}) copy-start(bf16[512,128]{1,0:T(8,128)(2,1)} %param.11) | copy-start | bytes 393220
  44.4 21.5 %copy-start.3 = (bf16[512]{0:T(512)(128)(2,1)S(1)}, bf16[512]{0:T(512)(128)(2,1)}, u32[]{:S(2)}) copy-start(bf16[512]{0:T(512)(128)(2,1)} %param.10) | copy-start | bytes 3076
  44.4 40.3 %all-to-all-start.2 = ((bf16[64,32,128]{2,1,0:T(8,128)(2,1)}), bf16[64,32,128]{2,1,0:T(8,128)(2,1)S(1)}, u32[]{:S(2)}, u32[]{:S(2)}) async-start(bf16[64,32,128]{2,1,0:T(8,128)(2,1)} %bitcast.7), calls=%async_computation.2 | async-start | bytes 1048576 | tf_op jit(solution)/shard_map/all_to_all | solution.py:194
  58.4 26.4 %copy-start = (bf16[8,128,512]{2,1,0:T(8,128)(2,1)}, bf16[8,128,512]{2,1,0:T(8,128)(2,1)S(1)}, u32[]{:S(2)}) copy-start(bf16[8,128,512]{2,1,0:T(8,128)(2,1)S(1)} %get-tuple-element.10.keep_ref) | copy-start | bytes 3145732
  58.4 29.9 %collective-permute-start.5 = (bf16[8,128,512]{2,1,0:T(8,128)(2,1)}, bf16[8,128,512]{2,1,0:T(8,128)(2,1)}, u32[]{:S(2)}, u32[]{:S(2)}) collective-permute-start(bf16[8,128,512]{2,1,0:T(8,128)(2,1)} %get-tuple-element.11), channel_id=1, source_target_pairs={{0,2},{1,3},{2,0},{3,1},{4,6},{5,7},{6,4},{7,5},{8,10},{9,11},{10,... | collective-permute-start | bytes 3145736 | tf_op jit(solution)/shard_map/ppermute | solution.py:31
  60.8 20.0 %collective-permute-start.1 = (bf16[2,16,32,128]{3,2,1,0:T(8,128)(2,1)S(1)}, bf16[2,16,32,128]{3,2,1,0:T(8,128)(2,1)S(1)}, u32[]{:S(2)}, u32[]{:S(2)}) collective-permute-start(bf16[2,16,32,128]{3,2,1,0:T(8,128)(2,1)S(1)} %pad_maximum_fusion.1), channel_id=1, source_target_pairs={{0,256},{1,257},{2,258},{3,259},{4,260},{5,261},{6,262},{7,263},{8... | collective-permute-start | bytes 786440 | tf_op jit(solution)/shard_map/ppermute | solution.py:31
  80.8 15.7 %collective-permute-start.3 = (bf16[4,16,32,128]{3,2,1,0:T(8,128)(2,1)S(1)}, bf16[4,16,32,128]{3,2,1,0:T(8,128)(2,1)}, u32[]{:S(2)}, u32[]{:S(2)}) collective-permute-start(bf16[4,16,32,128]{3,2,1,0:T(8,128)(2,1)S(1)} %pad_maximum_fusion.near_ref), channel_id=1, source_target_pairs={{0,128},{1,129},{2,130},{3,131},{4,132},{5,133},{6,134},{7,135},{8... | collective-permute-start | bytes 1572872 | tf_op jit(solution)/shard_map/ppermute | solution.py:31
  82.8 19.4 %collective-permute-start.2 = (bf16[4,16,32,128]{3,2,1,0:T(8,128)(2,1)S(1)}, bf16[4,16,32,128]{3,2,1,0:T(8,128)(2,1)S(1)}, u32[]{:S(2)}, u32[]{:S(2)}) collective-permute-start(bf16[4,16,32,128]{3,2,1,0:T(8,128)(2,1)S(1)} %pad_maximum_fusion.near_ref), channel_id=1, source_target_pairs={{0,16},{1,17},{2,18},{3,19},{4,20},{5,21},{6,22},{7,23},{8,24},{9,... | collective-permute-start | bytes 1572872 | tf_op jit(solution)/shard_map/ppermute | solution.py:31
  84.8 11.4 %collective-permute-start.6 = (f32[32,128]{1,0:T(8,128)S(1)}, f32[32,128]{1,0:T(8,128)S(1)}, u32[]{:S(2)}, u32[]{:S(2)}) collective-permute-start(f32[32,128]{1,0:T(8,128)S(1)} %get-tuple-element.37), channel_id=1, source_target_pairs={{0,16},{1,17},{2,18},{3,19},{4,20},{5,21},{6,22},{7,23},{8,24},{9,... | collective-permute-start | bytes 49160 | tf_op jit(solution)/shard_map/ppermute | solution.py:31
  88.3 1.2 copy-start.1
  92.0 37.6 %all-to-all-start.1 = ((bf16[8,128,512]{2,1,0:T(8,128)(2,1)}), bf16[8,128,512]{2,1,0:T(8,128)(2,1)}, u32[]{:S(2)}, u32[]{:S(2)}) async-start(bf16[8,128,512]{2,1,0:T(8,128)(2,1)} %shard_map.139), calls=%async_computation.1 | async-start | bytes 2097152 | tf_op jit(solution)/shard_map/all_to_all | solution.py:180
  96.5 5.6 %collective-permute-start.4 = (bf16[4,16,32,128]{3,2,1,0:T(8,128)(2,1)}, bf16[4,16,32,128]{3,2,1,0:T(8,128)(2,1)S(1)}, u32[]{:S(2)}, u32[]{:S(2)}) collective-permute-start(bf16[4,16,32,128]{3,2,1,0:T(8,128)(2,1)} %collective-permute-done.3.far_ref), channel_id=1, source_target_pairs={{0,16},{1,17},{2,18},{3,19},{4,20},{5,21},{6,22},{7,23},{8,24},{9,... | collective-permute-start | bytes 1572872 | tf_op jit(solution)/shard_map/ppermute | solution.py:31

commit v5 on v4

--- a/solution.py
+++ b/solution.py
@@ -33,6 +33,10 @@
 
 def x_near(z, y, c, x):
     return z, y, c, (x + (1 if (x + c) % 2 == 0 else -1)) % 8
+
+
+def y_half(z, y, c, x):
+    return z, (6, 7, 4, 5, 2, 3, 0, 1)[y], c, x
 
 
 def z_one(z, y, c, x):
@@ -111,11 +115,13 @@
     rows = groups * piece
     replica = lax.axis_index("replica")
     half = (replica + flip) % 2
+    y_half_index = lax.axis_index("fsdp") % 2
     acc = jnp.zeros((tok_ref.shape[0], hd), jnp.float32)
     for f in range(shards):
+        shard = (f % 8) * 2 + (y_half_index + f // 8) % 2
         for other, w_ref in enumerate(w_refs):
             quarter = (replica // 8 + other) % 2
-            start = pl.multiple_of(((f * 2 + half) * 2 + quarter) * rows, rows)
+            start = pl.multiple_of(((shard * 2 + half) * 2 + quarter) * rows, rows)
             acc = acc + jnp.dot(
                 tok_ref[:, pl.ds(start, rows)],
                 w_ref[:, f].reshape(rows, hd),
@@ -159,10 +165,15 @@
     gain_piece = lax.dynamic_slice_in_dim(norm_gain, order * piece, piece, 0).astype(jnp.float32)
     weight_piece = lax.dynamic_slice_in_dim(key_weight, order * piece, piece, 0).astype(jnp.float32)
     scaled_piece = (gain_piece[:, None] * weight_piece).astype(jnp.bfloat16)
-    shards = lax.axis_size("fsdp")
-    w_pieces = lax.all_to_all(
-        jnp.broadcast_to(scaled_piece[None], (shards, piece, hd)), "fsdp", 0, 0
-    )[None]
+    y_groups = [[2 * x + y for x in range(8)] for y in range(2)]
+    w_row = lax.all_to_all(
+        jnp.broadcast_to(scaled_piece[None], (8, piece, hd)),
+        "fsdp",
+        0,
+        0,
+        axis_index_groups=y_groups,
+    )
+    w_pieces = jnp.concatenate([w_row, permute(w_row, y_half)])[None]
 
     def doubled(values, move, bit):
         other = permute(values, move)

time: 133 us -> 134 us (level)
  the two profiles are of different devices: /device:TPU:16 before, /device:TPU:41 now
where the time goes in v5:
time: 134 us; the launch traced here: 133 us
  starting transfers between devices  61.5 us (46%)
  waiting for transfers between devices  37.7 us (28%)
  Pallas kernels  11.4 us (9%)
  blocking collectives  8.86 us (7%)
  local copies, waits for them, and re-layouts  6.02 us (4%)
  other arithmetic  5.42 us (4%)
  between operations  2.28 us (2%)
    ppermute x8, starting transfers between devices, permute(): return lax.ppermute(value, ALL, route(move))  37.3 us
    all_to_all x1, waiting for transfers between devices, step(): mine = lax.all_to_all(part, 'fsdp', 0, 0, axis_index_groups=x_groups)  23.6 us
    ppermute x8, waiting for transfers between devices, permute(): return lax.ppermute(value, ALL, route(move))  14.2 us
    all_to_all x1, starting transfers between devices, step(): inner_all = lax.all_to_all(halves, 'replica', 0, 0)  14.1 us
    all_to_all x1, starting transfers between devices, step(): mine = lax.all_to_all(part, 'fsdp', 0, 0, axis_index_groups=x_groups)  10.1 us
    all_to_all x1, blocking collectives, step(): lax.all_to_all(jnp.broadcast_to(scaled_piece[None], (8, piece, hd)), 'fsd...  8.86 us
    pallas_call x1, Pallas kernels, factor_parts(): pl.pallas_call(factor_kernel, out_shape=(pltpu.VMEM((tokens.shape[0], 128...  4.04 us
    pallas_call x1, Pallas kernels, step(): pl.pallas_call(keys_second, out_shape=out, in_specs=[VMEM] * 5, out_specs...  2.69 us
  transfers between devices with their start and end apart: 10, of which 3 were waited for; matrix products, arithmetic and copies ran while one was open for 4% of the time, Pallas kernels for 9%

profile of v5, /device:TPU:41, one launch (start us, length us, event | category | flops | bytes accessed | tf_op | source)
XLA Modules:
  0.0 133.1 jit_solution(13173759548686853220)
XLA Ops:
  0.7 0.8 dynamic-slice_convert_fusion
  1.5 0.8 multiply_convert_fusion
  2.3 8.9 %all_to_all.15 = bf16[8,32,128]{2,1,0:T(8,128)(2,1)S(1)} all-to-all(bf16[8,32,128]{2,1,0:T(8,128)(2,1)S(1)} %broadcast_in_dim.10), channel_id=1, replica_groups={{0,2,4,6,8,10,12,14},{1,3,5,7,9,11,13,15},{16,18,20,22,24,26,28,30},{17..., dimensions={0} | all-to-all | bytes 131072 | tf_op jit(solution)/shard_map/all_to_all | solution.py:169
  11.1 5.6 %collective-permute-start = (bf16[8,32,128]{2,1,0:T(8,128)(2,1)S(1)}, bf16[8,32,128]{2,1,0:T(8,128)(2,1)S(1)}, u32[]{:S(2)}, u32[]{:S(2)}) collective-permute-start(bf16[8,32,128]{2,1,0:T(8,128)(2,1)S(1)} %all_to_all.15), channel_id=1, source_target_pairs={{0,65},{1,64},{2,67},{3,66},{4,69},{5,68},{6,71},{7,70},{8,73},{9,... | collective-permute-start | bytes 196616 | tf_op jit(solution)/shard_map/ppermute | solution.py:31
  16.8 1.6 %collective-permute-done = bf16[8,32,128]{2,1,0:T(8,128)(2,1)S(1)} collective-permute-done((bf16[8,32,128]{2,1,0:T(8,128)(2,1)S(1)}, bf16[8,32,128]{2,1,0:T(8,128)(2,1)S(1)}, u32[]{:S(2)}, u32[]{:S(2)}) %collective-permute-start) | collective-permute-done | bytes 65568 | tf_op jit(solution)/shard_map/ppermute | solution.py:31
  18.4 14.3 %collective-permute-start.1 = (bf16[1,16,32,128]{3,2,1,0:T(8,128)(2,1)S(1)}, bf16[1,16,32,128]{3,2,1,0:T(8,128)(2,1)S(1)}, u32[]{:S(2)}, u32[]{:S(2)}) collective-permute-start(bf16[1,16,32,128]{3,2,1,0:T(8,128)(2,1)S(1)} %maximum_bitcast_fusion), channel_id=1, source_target_pairs={{0,512},{1,513},{2,514},{3,515},{4,516},{5,517},{6,518},{7,519},{8... | collective-permute-start | bytes 393224 | tf_op jit(solution)/shard_map/ppermute | solution.py:31
  33.4 1.0 dynamic-slice_reduce_fusion
  34.4 0.9 broadcast_in_dim.27
  35.3 0.0 copy-start.2
  35.3 0.0 copy-start.3
  35.3 14.1 %all-to-all-start.2 = ((bf16[64,32,128]{2,1,0:T(8,128)(2,1)}), bf16[64,32,128]{2,1,0:T(8,128)(2,1)S(1)}, u32[]{:S(2)}, u32[]{:S(2)}) async-start(bf16[64,32,128]{2,1,0:T(8,128)(2,1)} %bitcast.7), calls=%async_computation.2 | async-start | bytes 1048576 | tf_op jit(solution)/shard_map/all_to_all | solution.py:205
  49.4 4.0 %shard_map.136 = (f32[128,128]{1,0:T(8,128)S(1)}, bf16[8,128,512]{2,1,0:T(8,128)(2,1)S(1)}, bf16[8,128,512]{2,1,0:T(8,128)(2,1)}) custom-call(bf16[128,8192]{1,0:T(8,128)(2,1)} %tok_ref.5, bf16[128,128]{1,0:T(8,128)(2,1)} %cot_ref.1), custom_call_target="tpu_custom_call" | custom-call | tf_op jit(solution)/shard_map/pallas_call | solution.py:86
  53.5 0.0 copy-start
  53.5 4.2 %collective-permute-start.6 = (bf16[8,128,512]{2,1,0:T(8,128)(2,1)}, bf16[8,128,512]{2,1,0:T(8,128)(2,1)}, u32[]{:S(2)}, u32[]{:S(2)}) collective-permute-start(bf16[8,128,512]{2,1,0:T(8,128)(2,1)} %get-tuple-element.11), channel_id=1, source_target_pairs={{0,2},{1,3},{2,0},{3,1},{4,6},{5,7},{6,4},{7,5},{8,10},{9,11},{10,... | collective-permute-start | bytes 3145736 | tf_op jit(solution)/shard_map/ppermute | solution.py:31
  57.7 0.0 collective-permute-done.1
  57.8 4.0 %collective-permute-start.2 = (bf16[2,16,32,128]{3,2,1,0:T(8,128)(2,1)S(1)}, bf16[2,16,32,128]{3,2,1,0:T(8,128)(2,1)S(1)}, u32[]{:S(2)}, u32[]{:S(2)}) collective-permute-start(bf16[2,16,32,128]{3,2,1,0:T(8,128)(2,1)S(1)} %pad_maximum_fusion.1), channel_id=1, source_target_pairs={{0,256},{1,257},{2,258},{3,259},{4,260},{5,261},{6,262},{7,263},{8... | collective-permute-start | bytes 786440 | tf_op jit(solution)/shard_map/ppermute | solution.py:31
  61.8 0.8 constant_dynamic-slice_fusion.3
  62.6 0.0 copy-done.2
  62.6 0.1 copy.31
  62.7 0.0 copy-done.3
  63.5 12.5 %collective-permute-done.2 = bf16[2,16,32,128]{3,2,1,0:T(8,128)(2,1)S(1)} collective-permute-done((bf16[2,16,32,128]{3,2,1,0:T(8,128)(2,1)S(1)}, bf16[2,16,32,128]{3,2,1,0:T(8,128)(2,1)S(1)}, u32[]{:S(2)}, u32[]{:S(2)}) %collective-permute-start.2) | collective-permute-done | bytes 262176 | tf_op jit(solution)/shard_map/ppermute | solution.py:31
  76.1 1.9 %collective-permute-start.4 = (bf16[4,16,32,128]{3,2,1,0:T(8,128)(2,1)S(1)}, bf16[4,16,32,128]{3,2,1,0:T(8,128)(2,1)}, u32[]{:S(2)}, u32[]{:S(2)}) collective-permute-start(bf16[4,16,32,128]{3,2,1,0:T(8,128)(2,1)S(1)} %pad_maximum_fusion.near_ref), channel_id=1, source_target_pairs={{0,128},{1,129},{2,130},{3,131},{4,132},{5,133},{6,134},{7,135},{8... | collective-permute-start | bytes 1572872 | tf_op jit(solution)/shard_map/ppermute | solution.py:31
  78.0 2.3 %collective-permute-start.3 = (bf16[4,16,32,128]{3,2,1,0:T(8,128)(2,1)S(1)}, bf16[4,16,32,128]{3,2,1,0:T(8,128)(2,1)S(1)}, u32[]{:S(2)}, u32[]{:S(2)}) collective-permute-start(bf16[4,16,32,128]{3,2,1,0:T(8,128)(2,1)S(1)} %pad_maximum_fusion.near_ref), channel_id=1, source_target_pairs={{0,16},{1,17},{2,18},{3,19},{4,20},{5,21},{6,22},{7,23},{8,24},{9,... | collective-permute-start | bytes 1572872 | tf_op jit(solution)/shard_map/ppermute | solution.py:31
  80.3 0.0 all-to-all-done.2
  80.3 0.1 convert_reduce_fusion.1
  80.4 0.0 copy-done
  80.4 2.0 %collective-permute-start.7 = (f32[32,128]{1,0:T(8,128)S(1)}, f32[32,128]{1,0:T(8,128)S(1)}, u32[]{:S(2)}, u32[]{:S(2)}) collective-permute-start(f32[32,128]{1,0:T(8,128)S(1)} %get-tuple-element.37), channel_id=1, source_target_pairs={{0,16},{1,17},{2,18},{3,19},{4,20},{5,21},{6,22},{7,23},{8,24},{9,... | collective-permute-start | bytes 49160 | tf_op jit(solution)/shard_map/ppermute | solution.py:31
  82.5 0.5 constant_dynamic-slice_fusion.1
  83.0 0.5 constant_dynamic-slice_fusion
  83.5 0.0 collective-permute-done.6.other_ref
  83.5 0.0 copy-start.1
  83.5 1.2 copy-done.1
  84.8 2.5 %shard_map.139 = bf16[8,128,512]{2,1,0:T(8,128)(2,1)} custom-call(bf16[8,128,512]{2,1,0:T(8,128)(2,1)S(1)} %copy-done.1, bf16[8,128,512]{2,1,0:T(8,128)(2,1)} %collective-permute-done.6.other_ref), custom_call_target="tpu_custom_call" | custom-call | tf_op jit(solution)/shard_map/pallas_call | solution.py:105
  87.2 10.1 %all-to-all-start.1 = ((bf16[8,128,512]{2,1,0:T(8,128)(2,1)}), bf16[8,128,512]{2,1,0:T(8,128)(2,1)}, u32[]{:S(2)}, u32[]{:S(2)}) async-start(bf16[8,128,512]{2,1,0:T(8,128)(2,1)} %shard_map.139), calls=%async_computation.1 | async-start | bytes 2097152 | tf_op jit(solution)/shard_map/all_to_all | solution.py:191
  97.3 0.0 collective-permute-done.7
  97.4 0.0 collective-permute-done.4.far_ref
  97.4 2.9 %collective-permute-start.5 = (bf16[4,16,32,128]{3,2,1,0:T(8,128)(2,1)}, bf16[4,16,32,128]{3,2,1,0:T(8,128)(2,1)S(1)}, u32[]{:S(2)}, u32[]{:S(2)}) collective-permute-start(bf16[4,16,32,128]{3,2,1,0:T(8,128)(2,1)} %collective-permute-done.4.far_ref), channel_id=1, source_target_pairs={{0,16},{1,17},{2,18},{3,19},{4,20},{5,21},{6,22},{7,23},{8,24},{9,... | collective-permute-start | bytes 1572872 | tf_op jit(solution)/shard_map/ppermute | solution.py:31
  100.3 1.6 %fusion.3 = bf16[1,1,8192]{2,1,0:T(2,128)(2,1)} fusion(f32[1,1,8192]{2,1,0:T(1,128)S(1)} %bitcast.45, bf16[1,32,1,8192]{3,1,2,0:T(8,128)(2,1)} %param.15, s32[]{:T(128)S(6)} %select_n.102, f32[]{:T(128)S(6)} %sub.37), kind=kLoop, calls=%fused_computation.16 | loop fusion | flops 32768 | bytes 65544 | tf_op jit(solution)/shard_map/convert_element_type | solution.py:222
  101.8 2.2 %shard_map.137.first_ref = f32[128,128]{1,0:T(8,128)S(1)} custom-call(bf16[128,8192]{1,0:T(8,128)(2,1)} %tok_ref.5, bf16[4,16,32,128]{3,2,1,0:T(8,128)(2,1)S(1)} %pad_maximum_fusion.near_ref, bf16[4,16,32,128]{3,2,1,0:T(8,128)(2,1)} %collective-permute-done.4.far_ref), custom_call_target="tpu_custom_call" | custom-call | tf_op jit(solution)/shard_map/pallas_call | solution.py:225
  104.0 0.0 collective-permute-done.3.near_ref
  104.0 0.0 collective-permute-done.5.far_ref
  104.0 2.7 %shard_map.138 = bf16[128,128]{1,0:T(8,128)(2,1)} custom-call(bf16[128,8192]{1,0:T(8,128)(2,1)} %tok_ref.5, bf16[4,16,32,128]{3,2,1,0:T(8,128)(2,1)S(1)} %collective-permute-done.3.near_ref, bf16[4,16,32,128]{3,2,1,0:T(8,128)(2,1)S(1)} %collective-permute-done.5.far_ref, f32[128,128]{1,0:T(8,128)S(1)} %get-tuple-element.9.inv_ref, ...), custom_call_target="tpu_custom_call" | custom-call | tf_op jit(solution)/shard_map/pallas_call | solution.py:231
  106.7 23.6 %all-to-all-done.1 = bf16[8,128,512]{2,1,0:T(8,128)(2,1)} async-done(((bf16[8,128,512]{2,1,0:T(8,128)(2,1)}), bf16[8,128,512]{2,1,0:T(8,128)(2,1)}, u32[]{:S(2)}, u32[]{:S(2)}) %all-to-all-start.1) | async-done | bytes 1048608 | tf_op jit(solution)/shard_map/all_to_all | solution.py:191
  130.3 1.4 %convert_reduce_fusion = f32[128,512]{1,0:T(8,128)S(1)} fusion(bf16[8,128,512]{2,1,0:T(8,128)(2,1)} %all-to-all-done.1), kind=kLoop, calls=%fused_computation | loop fusion | flops 983040 | bytes 1310720 | tf_op jit(solution)/shard_map/reduce_sum | solution.py:235
  131.7 0.6 fusion.1
  132.3 0.8 copy.36
  (14 shorter events, 0.3 us)
Async XLA Ops:
  11.1 7.3 %collective-permute-start = (bf16[8,32,128]{2,1,0:T(8,128)(2,1)S(1)}, bf16[8,32,128]{2,1,0:T(8,128)(2,1)S(1)}, u32[]{:S(2)}, u32[]{:S(2)}) collective-permute-start(bf16[8,32,128]{2,1,0:T(8,128)(2,1)S(1)} %all_to_all.15), channel_id=1, source_target_pairs={{0,65},{1,64},{2,67},{3,66},{4,69},{5,68},{6,71},{7,70},{8,73},{9,... | collective-permute-start | bytes 196616 | tf_op jit(solution)/shard_map/ppermute | solution.py:31
  18.4 39.3 %collective-permute-start.1 = (bf16[1,16,32,128]{3,2,1,0:T(8,128)(2,1)S(1)}, bf16[1,16,32,128]{3,2,1,0:T(8,128)(2,1)S(1)}, u32[]{:S(2)}, u32[]{:S(2)}) collective-permute-start(bf16[1,16,32,128]{3,2,1,0:T(8,128)(2,1)S(1)} %maximum_bitcast_fusion), channel_id=1, source_target_pairs={{0,512},{1,513},{2,514},{3,515},{4,516},{5,517},{6,518},{7,519},{8... | collective-permute-start | bytes 393224 | tf_op jit(solution)/shard_map/ppermute | solution.py:31
  35.3 27.3 %copy-start.2 = (bf16[512,128]{1,0:T(8,128)(2,1)S(1)}, bf16[512,128]{1,0:T(8,128)(2,1)}, u32[]{:S(2)}) copy-start(bf16[512,128]{1,0:T(8,128)(2,1)} %param.11) | copy-start | bytes 393220
  35.3 27.4 %copy-start.3 = (bf16[512]{0:T(512)(128)(2,1)S(1)}, bf16[512]{0:T(512)(128)(2,1)}, u32[]{:S(2)}) copy-start(bf16[512]{0:T(512)(128)(2,1)} %param.10) | copy-start | bytes 3076
  35.3 45.0 %all-to-all-start.2 = ((bf16[64,32,128]{2,1,0:T(8,128)(2,1)}), bf16[64,32,128]{2,1,0:T(8,128)(2,1)S(1)}, u32[]{:S(2)}, u32[]{:S(2)}) async-start(bf16[64,32,128]{2,1,0:T(8,128)(2,1)} %bitcast.7), calls=%async_computation.2 | async-start | bytes 1048576 | tf_op jit(solution)/shard_map/all_to_all | solution.py:205
  53.5 26.9 %copy-start = (bf16[8,128,512]{2,1,0:T(8,128)(2,1)}, bf16[8,128,512]{2,1,0:T(8,128)(2,1)S(1)}, u32[]{:S(2)}) copy-start(bf16[8,128,512]{2,1,0:T(8,128)(2,1)S(1)} %get-tuple-element.10.keep_ref) | copy-start | bytes 3145732
  53.5 30.1 %collective-permute-start.6 = (bf16[8,128,512]{2,1,0:T(8,128)(2,1)}, bf16[8,128,512]{2,1,0:T(8,128)(2,1)}, u32[]{:S(2)}, u32[]{:S(2)}) collective-permute-start(bf16[8,128,512]{2,1,0:T(8,128)(2,1)} %get-tuple-element.11), channel_id=1, source_target_pairs={{0,2},{1,3},{2,0},{3,1},{4,6},{5,7},{6,4},{7,5},{8,10},{9,11},{10,... | collective-permute-start | bytes 3145736 | tf_op jit(solution)/shard_map/ppermute | solution.py:31
  57.8 18.2 %collective-permute-start.2 = (bf16[2,16,32,128]{3,2,1,0:T(8,128)(2,1)S(1)}, bf16[2,16,32,128]{3,2,1,0:T(8,128)(2,1)S(1)}, u32[]{:S(2)}, u32[]{:S(2)}) collective-permute-start(bf16[2,16,32,128]{3,2,1,0:T(8,128)(2,1)S(1)} %pad_maximum_fusion.1), channel_id=1, source_target_pairs={{0,256},{1,257},{2,258},{3,259},{4,260},{5,261},{6,262},{7,263},{8... | collective-permute-start | bytes 786440 | tf_op jit(solution)/shard_map/ppermute | solution.py:31
  76.1 21.3 %collective-permute-start.4 = (bf16[4,16,32,128]{3,2,1,0:T(8,128)(2,1)S(1)}, bf16[4,16,32,128]{3,2,1,0:T(8,128)(2,1)}, u32[]{:S(2)}, u32[]{:S(2)}) collective-permute-start(bf16[4,16,32,128]{3,2,1,0:T(8,128)(2,1)S(1)} %pad_maximum_fusion.near_ref), channel_id=1, source_target_pairs={{0,128},{1,129},{2,130},{3,131},{4,132},{5,133},{6,134},{7,135},{8... | collective-permute-start | bytes 1572872 | tf_op jit(solution)/shard_map/ppermute | solution.py:31
  78.0 26.0 %collective-permute-start.3 = (bf16[4,16,32,128]{3,2,1,0:T(8,128)(2,1)S(1)}, bf16[4,16,32,128]{3,2,1,0:T(8,128)(2,1)S(1)}, u32[]{:S(2)}, u32[]{:S(2)}) collective-permute-start(bf16[4,16,32,128]{3,2,1,0:T(8,128)(2,1)S(1)} %pad_maximum_fusion.near_ref), channel_id=1, source_target_pairs={{0,16},{1,17},{2,18},{3,19},{4,20},{5,21},{6,22},{7,23},{8,24},{9,... | collective-permute-start | bytes 1572872 | tf_op jit(solution)/shard_map/ppermute | solution.py:31
  80.4 16.9 %collective-permute-start.7 = (f32[32,128]{1,0:T(8,128)S(1)}, f32[32,128]{1,0:T(8,128)S(1)}, u32[]{:S(2)}, u32[]{:S(2)}) collective-permute-start(f32[32,128]{1,0:T(8,128)S(1)} %get-tuple-element.37), channel_id=1, source_target_pairs={{0,16},{1,17},{2,18},{3,19},{4,20},{5,21},{6,22},{7,23},{8,24},{9,... | collective-permute-start | bytes 49160 | tf_op jit(solution)/shard_map/ppermute | solution.py:31
  83.5 1.2 copy-start.1
  87.2 43.0 %all-to-all-start.1 = ((bf16[8,128,512]{2,1,0:T(8,128)(2,1)}), bf16[8,128,512]{2,1,0:T(8,128)(2,1)}, u32[]{:S(2)}, u32[]{:S(2)}) async-start(bf16[8,128,512]{2,1,0:T(8,128)(2,1)} %shard_map.139), calls=%async_computation.1 | async-start | bytes 2097152 | tf_op jit(solution)/shard_map/all_to_all | solution.py:191
  97.4 6.6 %collective-permute-start.5 = (bf16[4,16,32,128]{3,2,1,0:T(8,128)(2,1)}, bf16[4,16,32,128]{3,2,1,0:T(8,128)(2,1)S(1)}, u32[]{:S(2)}, u32[]{:S(2)}) collective-permute-start(bf16[4,16,32,128]{3,2,1,0:T(8,128)(2,1)} %collective-permute-done.4.far_ref), channel_id=1, source_target_pairs={{0,16},{1,17},{2,18},{3,19},{4,20},{5,21},{6,22},{7,23},{8,24},{9,... | collective-permute-start | bytes 1572872 | tf_op jit(solution)/shard_map/ppermute | solution.py:31

commit v6 on v5

--- a/solution.py
+++ b/solution.py
@@ -40,11 +40,11 @@
 
 
 def z_one(z, y, c, x):
-    return z ^ 1, y, c, x
+    return (z + (1 if (z + c) % 2 == 0 else -1)) % 8, y, c, x
 
 
 def z_two(z, y, c, x):
-    return z ^ 2, y, c, x
+    return z ^ (6 if c else 2), y, c, x
 
 
 def z_four(z, y, c, x):
@@ -110,17 +110,17 @@
     )(*on_chip(keep, other))
 
 
-def keys_product(tok_ref, w_refs, flip):
-    groups, shards, piece, hd = w_refs[0].shape
+def keys_product(tok_ref, parts):
+    groups, shards, piece, hd = parts[0][0].shape
     rows = groups * piece
     replica = lax.axis_index("replica")
-    half = (replica + flip) % 2
     y_half_index = lax.axis_index("fsdp") % 2
     acc = jnp.zeros((tok_ref.shape[0], hd), jnp.float32)
     for f in range(shards):
         shard = (f % 8) * 2 + (y_half_index + f // 8) % 2
-        for other, w_ref in enumerate(w_refs):
-            quarter = (replica // 8 + other) % 2
+        for w_ref, flip_core, flip_plane in parts:
+            half = (replica + flip_core) % 2
+            quarter = (replica // 8 + flip_plane) % 2
             start = pl.multiple_of(((shard * 2 + half) * 2 + quarter) * rows, rows)
             acc = acc + jnp.dot(
                 tok_ref[:, pl.ds(start, rows)],
@@ -130,12 +130,17 @@
     return acc
 
 
-def keys_first(tok_ref, near_ref, far_ref, out_ref):
-    out_ref[...] = keys_product(tok_ref, (near_ref, far_ref), 0)
-
-
-def keys_second(tok_ref, near_ref, far_ref, inv_ref, first_ref, out_ref):
-    acc = first_ref[...] + keys_product(tok_ref, (near_ref, far_ref), 1)
+def keys_near(tok_ref, near_ref, out_ref):
+    out_ref[...] = keys_product(tok_ref, ((near_ref, 0, 0),))
+
+
+def keys_mid(tok_ref, far_ref, near_other_ref, so_far_ref, out_ref):
+    acc = keys_product(tok_ref, ((far_ref, 0, 1), (near_other_ref, 1, 0)))
+    out_ref[...] = so_far_ref[...] + acc
+
+
+def keys_last(tok_ref, far_other_ref, inv_ref, so_far_ref, out_ref):
+    acc = so_far_ref[...] + keys_product(tok_ref, ((far_other_ref, 1, 1),))
     out_ref[...] = (acc * inv_ref[...]).astype(out_ref.dtype)
 
 
@@ -222,15 +227,16 @@
     new_inner = new_inner.astype(jnp.bfloat16).reshape(1, -1)
 
     out = jax.ShapeDtypeStruct((tokens.shape[0], hd), jnp.bfloat16)
-    first = pl.pallas_call(
-        keys_first,
-        out_shape=pltpu.VMEM(out.shape, jnp.float32),
-        in_specs=[VMEM] * 3,
-        out_specs=VMEM,
-    )(tokens, *on_chip(w_near, w_far))
-    key_out = pl.pallas_call(
-        keys_second, out_shape=out, in_specs=[VMEM] * 5, out_specs=VMEM
-    )(tokens, *on_chip(w_near_other, w_far_other, inv, first))
+    so_far = pltpu.VMEM(out.shape, jnp.float32)
+
+    def keys(kernel, shape, *values):
+        return pl.pallas_call(
+            kernel, out_shape=shape, in_specs=[VMEM] * (1 + len(values)), out_specs=VMEM
+        )(tokens, *on_chip(*values))
+
+    part_keys = keys(keys_near, so_far, w_near)
+    part_keys = keys(keys_mid, so_far, w_far, w_near_other, part_keys)
+    key_out = keys(keys_last, out, w_far_other, inv, part_keys)
 
     factor = jnp.sum(mine.astype(jnp.float32), axis=0).T
     weight_grad = norm_gain.astype(jnp.float32)[:, None] * factor

time: 134 us -> 134 us (level)
  the two profiles are of different devices: /device:TPU:41 before, /device:TPU:1 now
where the time goes in v6:
time: 134 us; the launch traced here: 133 us
  starting transfers between devices  57.8 us (43%)
  waiting for transfers between devices  33.1 us (25%)
  blocking collectives  14.3 us (11%)
  Pallas kernels  13.1 us (10%)
  other arithmetic  6.47 us (5%)
  local copies, waits for them, and re-layouts  6.04 us (5%)
  between operations  2.28 us (2%)
    ppermute x8, starting transfers between devices, permute(): return lax.ppermute(value, ALL, route(move))  38 us
    all_to_all x1, waiting for transfers between devices, step(): mine = lax.all_to_all(part, 'fsdp', 0, 0, axis_index_groups=x_groups)  24.6 us
    all_to_all x1, blocking collectives, step(): lax.all_to_all(jnp.broadcast_to(scaled_piece[None], (8, piece, hd)), 'fsd...  14.3 us
    all_to_all x1, starting transfers between devices, step(): inner_all = lax.all_to_all(halves, 'replica', 0, 0)  13.8 us
    ppermute x8, waiting for transfers between devices, permute(): return lax.ppermute(value, ALL, route(move))  8.43 us
    pallas_call x3, Pallas kernels, keys(): pl.pallas_call(kernel, out_shape=shape, in_specs=[VMEM] * (1 + len(values...  6.59 us
    all_to_all x1, starting transfers between devices, step(): mine = lax.all_to_all(part, 'fsdp', 0, 0, axis_index_groups=x_groups)  6.04 us
    pallas_call x1, Pallas kernels, factor_parts(): pl.pallas_call(factor_kernel, out_shape=(pltpu.VMEM((tokens.shape[0], 128...  4.04 us
  transfers between devices with their start and end apart: 10, of which 3 were waited for; matrix products, arithmetic and copies ran while one was open for 5% of the time, Pallas kernels for 10%

profile of v6, /device:TPU:1, one launch (start us, length us, event | category | flops | bytes accessed | tf_op | source)
XLA Modules:
  0.0 133.1 jit_solution(15084635458285015889)
XLA Ops:
  0.7 0.8 dynamic-slice_convert_fusion
  1.5 0.8 multiply_convert_fusion
  2.3 14.3 %all_to_all.15 = bf16[8,32,128]{2,1,0:T(8,128)(2,1)S(1)} all-to-all(bf16[8,32,128]{2,1,0:T(8,128)(2,1)S(1)} %broadcast_in_dim.10), channel_id=1, replica_groups={{0,2,4,6,8,10,12,14},{1,3,5,7,9,11,13,15},{16,18,20,22,24,26,28,30},{17..., dimensions={0} | all-to-all | bytes 131072 | tf_op jit(solution)/shard_map/all_to_all | solution.py:174
  16.6 6.6 %collective-permute-start = (bf16[8,32,128]{2,1,0:T(8,128)(2,1)S(1)}, bf16[8,32,128]{2,1,0:T(8,128)(2,1)S(1)}, u32[]{:S(2)}, u32[]{:S(2)}) collective-permute-start(bf16[8,32,128]{2,1,0:T(8,128)(2,1)S(1)} %all_to_all.15), channel_id=1, source_target_pairs={{0,65},{1,64},{2,67},{3,66},{4,69},{5,68},{6,71},{7,70},{8,73},{9,... | collective-permute-start | bytes 196616 | tf_op jit(solution)/shard_map/ppermute | solution.py:31
  23.2 1.9 %collective-permute-done = bf16[8,32,128]{2,1,0:T(8,128)(2,1)S(1)} collective-permute-done((bf16[8,32,128]{2,1,0:T(8,128)(2,1)S(1)}, bf16[8,32,128]{2,1,0:T(8,128)(2,1)S(1)}, u32[]{:S(2)}, u32[]{:S(2)}) %collective-permute-start) | collective-permute-done | bytes 65568 | tf_op jit(solution)/shard_map/ppermute | solution.py:31
  25.1 14.2 %collective-permute-start.1 = (bf16[1,16,32,128]{3,2,1,0:T(8,128)(2,1)S(1)}, bf16[1,16,32,128]{3,2,1,0:T(8,128)(2,1)S(1)}, u32[]{:S(2)}, u32[]{:S(2)}) collective-permute-start(bf16[1,16,32,128]{3,2,1,0:T(8,128)(2,1)S(1)} %maximum_bitcast_fusion), channel_id=1, source_target_pairs={{0,512},{1,513},{2,514},{3,515},{4,516},{5,517},{6,518},{7,519},{8... | collective-permute-start | bytes 393224 | tf_op jit(solution)/shard_map/ppermute | solution.py:31
  40.0 1.0 dynamic-slice_reduce_fusion
  41.0 0.9 broadcast_in_dim.27
  41.9 0.0 copy-start.2
  41.9 0.0 copy-start.3
  41.9 13.8 %all-to-all-start.2 = ((bf16[64,32,128]{2,1,0:T(8,128)(2,1)}), bf16[64,32,128]{2,1,0:T(8,128)(2,1)}, u32[]{:S(2)}, u32[]{:S(2)}) async-start(bf16[64,32,128]{2,1,0:T(8,128)(2,1)} %bitcast.7), calls=%async_computation.2 | async-start | bytes 1048576 | tf_op jit(solution)/shard_map/all_to_all | solution.py:210
  55.8 4.0 %shard_map.136 = (f32[128,128]{1,0:T(8,128)S(1)}, bf16[8,128,512]{2,1,0:T(8,128)(2,1)S(1)}, bf16[8,128,512]{2,1,0:T(8,128)(2,1)}) custom-call(bf16[128,8192]{1,0:T(8,128)(2,1)} %tok_ref.7, bf16[128,128]{1,0:T(8,128)(2,1)} %cot_ref.1), custom_call_target="tpu_custom_call" | custom-call | tf_op jit(solution)/shard_map/pallas_call | solution.py:86
  59.8 0.0 copy-start
  59.8 1.9 %collective-permute-start.6 = (bf16[8,128,512]{2,1,0:T(8,128)(2,1)}, bf16[8,128,512]{2,1,0:T(8,128)(2,1)}, u32[]{:S(2)}, u32[]{:S(2)}) collective-permute-start(bf16[8,128,512]{2,1,0:T(8,128)(2,1)} %get-tuple-element.11), channel_id=1, source_target_pairs={{0,2},{1,3},{2,0},{3,1},{4,6},{5,7},{6,4},{7,5},{8,10},{9,11},{10,... | collective-permute-start | bytes 3145736 | tf_op jit(solution)/shard_map/ppermute | solution.py:31
  61.7 0.0 collective-permute-done.1
  61.8 5.6 %collective-permute-start.2 = (bf16[2,16,32,128]{3,2,1,0:T(8,128)(2,1)S(1)}, bf16[2,16,32,128]{3,2,1,0:T(8,128)(2,1)S(1)}, u32[]{:S(2)}, u32[]{:S(2)}) collective-permute-start(bf16[2,16,32,128]{3,2,1,0:T(8,128)(2,1)S(1)} %pad_maximum_fusion.1), channel_id=1, source_target_pairs={{0,256},{1,257},{2,258},{3,259},{4,260},{5,261},{6,262},{7,263},{8... | collective-permute-start | bytes 786440 | tf_op jit(solution)/shard_map/ppermute | solution.py:31
  67.4 0.8 constant_dynamic-slice_fusion.3
  68.2 0.0 copy-done.2
  68.2 0.1 copy.31
  68.3 0.0 copy-done.3
  69.0 6.5 %collective-permute-done.2 = bf16[2,16,32,128]{3,2,1,0:T(8,128)(2,1)S(1)} collective-permute-done((bf16[2,16,32,128]{3,2,1,0:T(8,128)(2,1)S(1)}, bf16[2,16,32,128]{3,2,1,0:T(8,128)(2,1)S(1)}, u32[]{:S(2)}, u32[]{:S(2)}) %collective-permute-start.2) | collective-permute-done | bytes 262176 | tf_op jit(solution)/shard_map/ppermute | solution.py:31
  75.6 0.0 copy-done
  75.6 3.0 %collective-permute-start.3 = (bf16[4,16,32,128]{3,2,1,0:T(8,128)(2,1)S(1)}, bf16[4,16,32,128]{3,2,1,0:T(8,128)(2,1)S(1)}, u32[]{:S(2)}, u32[]{:S(2)}) collective-permute-start(bf16[4,16,32,128]{3,2,1,0:T(8,128)(2,1)S(1)} %pad_maximum_fusion.near_ref), channel_id=1, source_target_pairs={{0,128},{1,129},{2,130},{3,131},{4,132},{5,133},{6,134},{7,135},{8... | collective-permute-start | bytes 1572872 | tf_op jit(solution)/shard_map/ppermute | solution.py:31
  78.7 2.6 %collective-permute-start.5 = (bf16[4,16,32,128]{3,2,1,0:T(8,128)(2,1)S(1)}, bf16[4,16,32,128]{3,2,1,0:T(8,128)(2,1)}, u32[]{:S(2)}, u32[]{:S(2)}) collective-permute-start(bf16[4,16,32,128]{3,2,1,0:T(8,128)(2,1)S(1)} %pad_maximum_fusion.near_ref), channel_id=1, source_target_pairs={{0,16},{1,17},{2,18},{3,19},{4,20},{5,21},{6,22},{7,23},{8,24},{9,... | collective-permute-start | bytes 1572872 | tf_op jit(solution)/shard_map/ppermute | solution.py:31
  81.2 1.9 %shard_map.137.so_far_ref = f32[128,128]{1,0:T(8,128)S(1)} custom-call(bf16[128,8192]{1,0:T(8,128)(2,1)} %tok_ref.7, bf16[4,16,32,128]{3,2,1,0:T(8,128)(2,1)S(1)} %pad_maximum_fusion.near_ref), custom_call_target="tpu_custom_call" | custom-call | tf_op jit(solution)/shard_map/pallas_call | solution.py:233
  83.2 0.0 all-to-all-done.2
  83.2 1.1 convert_reduce_fusion.1
  84.3 1.9 %collective-permute-start.7 = (f32[32,128]{1,0:T(8,128)S(1)}, f32[32,128]{1,0:T(8,128)S(1)}, u32[]{:S(2)}, u32[]{:S(2)}) collective-permute-start(f32[32,128]{1,0:T(8,128)S(1)} %get-tuple-element.37), channel_id=1, source_target_pairs={{0,16},{1,17},{2,18},{3,19},{4,20},{5,21},{6,22},{7,23},{8,24},{9,... | collective-permute-start | bytes 49160 | tf_op jit(solution)/shard_map/ppermute | solution.py:31
  86.3 0.5 constant_dynamic-slice_fusion.1
  86.8 0.5 constant_dynamic-slice_fusion
  87.3 0.0 collective-permute-done.6.other_ref
  87.3 0.0 copy-start.1
  87.3 1.2 copy-done.1
  88.5 2.5 %shard_map.140 = bf16[8,128,512]{2,1,0:T(8,128)(2,1)} custom-call(bf16[8,128,512]{2,1,0:T(8,128)(2,1)S(1)} %copy-done.1, bf16[8,128,512]{2,1,0:T(8,128)(2,1)} %collective-permute-done.6.other_ref), custom_call_target="tpu_custom_call" | custom-call | tf_op jit(solution)/shard_map/pallas_call | solution.py:105
  91.0 6.0 %all-to-all-start.1 = ((bf16[8,128,512]{2,1,0:T(8,128)(2,1)}), bf16[8,128,512]{2,1,0:T(8,128)(2,1)}, u32[]{:S(2)}, u32[]{:S(2)}) async-start(bf16[8,128,512]{2,1,0:T(8,128)(2,1)} %shard_map.140), calls=%async_computation.1 | async-start | bytes 2097152 | tf_op jit(solution)/shard_map/all_to_all | solution.py:196
  97.1 0.0 collective-permute-done.7
  97.1 0.0 collective-permute-done.3.far_ref
  97.1 2.2 %collective-permute-start.4 = (bf16[4,16,32,128]{3,2,1,0:T(8,128)(2,1)S(1)}, bf16[4,16,32,128]{3,2,1,0:T(8,128)(2,1)S(1)}, u32[]{:S(2)}, u32[]{:S(2)}) collective-permute-start(bf16[4,16,32,128]{3,2,1,0:T(8,128)(2,1)S(1)} %collective-permute-done.3.far_ref), channel_id=1, source_target_pairs={{0,16},{1,17},{2,18},{3,19},{4,20},{5,21},{6,22},{7,23},{8,24},{9,... | collective-permute-start | bytes 1572872 | tf_op jit(solution)/shard_map/ppermute | solution.py:31
  99.3 1.6 %fusion.3 = bf16[1,1,8192]{2,1,0:T(2,128)(2,1)} fusion(f32[1,1,8192]{2,1,0:T(1,128)S(1)} %bitcast.45, bf16[1,32,1,8192]{3,1,2,0:T(8,128)(2,1)} %param.15, s32[]{:T(128)S(6)} %select_n.102, f32[]{:T(128)S(6)} %sub.37), kind=kLoop, calls=%fused_computation.16 | loop fusion | flops 32768 | bytes 65544 | tf_op jit(solution)/shard_map/convert_element_type | solution.py:227
  100.9 0.0 collective-permute-done.5.near_other_ref
  100.9 2.2 %shard_map.138.so_far_ref = f32[128,128]{1,0:T(8,128)S(1)} custom-call(bf16[128,8192]{1,0:T(8,128)(2,1)} %tok_ref.7, bf16[4,16,32,128]{3,2,1,0:T(8,128)(2,1)S(1)} %collective-permute-done.3.far_ref, bf16[4,16,32,128]{3,2,1,0:T(8,128)(2,1)} %collective-permute-done.5.near_other_ref, f32[128,128]{1,0:T(8,128)S(1)} %shard_map.137.so_far_ref), custom_call_target="tpu_custom_call" | custom-call | tf_op jit(solution)/shard_map/pallas_call | solution.py:233
  103.1 0.0 collective-permute-done.4.far_other_ref
  103.1 2.5 %shard_map.139 = bf16[128,128]{1,0:T(8,128)(2,1)} custom-call(bf16[128,8192]{1,0:T(8,128)(2,1)} %tok_ref.7, bf16[4,16,32,128]{3,2,1,0:T(8,128)(2,1)S(1)} %collective-permute-done.4.far_other_ref, f32[128,128]{1,0:T(8,128)S(1)} %get-tuple-element.9.inv_ref, f32[128,128]{1,0:T(8,128)S(1)} %shard_map.138.so_far_ref), custom_call_target="tpu_custom_call" | custom-call | tf_op jit(solution)/shard_map/pallas_call | solution.py:233
  105.6 24.6 %all-to-all-done.1 = bf16[8,128,512]{2,1,0:T(8,128)(2,1)} async-done(((bf16[8,128,512]{2,1,0:T(8,128)(2,1)}), bf16[8,128,512]{2,1,0:T(8,128)(2,1)}, u32[]{:S(2)}, u32[]{:S(2)}) %all-to-all-start.1) | async-done | bytes 1048608 | tf_op jit(solution)/shard_map/all_to_all | solution.py:196
  130.3 1.4 %convert_reduce_fusion = f32[128,512]{1,0:T(8,128)S(1)} fusion(bf16[8,128,512]{2,1,0:T(8,128)(2,1)} %all-to-all-done.1), kind=kLoop, calls=%fused_computation | loop fusion | flops 983040 | bytes 1310720 | tf_op jit(solution)/shard_map/reduce_sum | solution.py:241
  131.7 0.6 fusion.1
  132.3 0.8 copy.36
  (14 shorter events, 0.3 us)
Async XLA Ops:
  16.6 8.5 %collective-permute-start = (bf16[8,32,128]{2,1,0:T(8,128)(2,1)S(1)}, bf16[8,32,128]{2,1,0:T(8,128)(2,1)S(1)}, u32[]{:S(2)}, u32[]{:S(2)}) collective-permute-start(bf16[8,32,128]{2,1,0:T(8,128)(2,1)S(1)} %all_to_all.15), channel_id=1, source_target_pairs={{0,65},{1,64},{2,67},{3,66},{4,69},{5,68},{6,71},{7,70},{8,73},{9,... | collective-permute-start | bytes 196616 | tf_op jit(solution)/shard_map/ppermute | solution.py:31
  25.1 36.6 %collective-permute-start.1 = (bf16[1,16,32,128]{3,2,1,0:T(8,128)(2,1)S(1)}, bf16[1,16,32,128]{3,2,1,0:T(8,128)(2,1)S(1)}, u32[]{:S(2)}, u32[]{:S(2)}) collective-permute-start(bf16[1,16,32,128]{3,2,1,0:T(8,128)(2,1)S(1)} %maximum_bitcast_fusion), channel_id=1, source_target_pairs={{0,512},{1,513},{2,514},{3,515},{4,516},{5,517},{6,518},{7,519},{8... | collective-permute-start | bytes 393224 | tf_op jit(solution)/shard_map/ppermute | solution.py:31
  41.9 26.2 %copy-start.2 = (bf16[512,128]{1,0:T(8,128)(2,1)S(1)}, bf16[512,128]{1,0:T(8,128)(2,1)}, u32[]{:S(2)}) copy-start(bf16[512,128]{1,0:T(8,128)(2,1)} %param.11) | copy-start | bytes 393220
  41.9 26.4 %copy-start.3 = (bf16[512]{0:T(512)(128)(2,1)S(1)}, bf16[512]{0:T(512)(128)(2,1)}, u32[]{:S(2)}) copy-start(bf16[512]{0:T(512)(128)(2,1)} %param.10) | copy-start | bytes 3076
  41.9 41.2 %all-to-all-start.2 = ((bf16[64,32,128]{2,1,0:T(8,128)(2,1)}), bf16[64,32,128]{2,1,0:T(8,128)(2,1)}, u32[]{:S(2)}, u32[]{:S(2)}) async-start(bf16[64,32,128]{2,1,0:T(8,128)(2,1)} %bitcast.7), calls=%async_computation.2 | async-start | bytes 1048576 | tf_op jit(solution)/shard_map/all_to_all | solution.py:210
  59.8 15.8 %copy-start = (bf16[8,128,512]{2,1,0:T(8,128)(2,1)}, bf16[8,128,512]{2,1,0:T(8,128)(2,1)S(1)}, u32[]{:S(2)}) copy-start(bf16[8,128,512]{2,1,0:T(8,128)(2,1)S(1)} %get-tuple-element.10.keep_ref) | copy-start | bytes 3145732
  59.8 27.5 %collective-permute-start.6 = (bf16[8,128,512]{2,1,0:T(8,128)(2,1)}, bf16[8,128,512]{2,1,0:T(8,128)(2,1)}, u32[]{:S(2)}, u32[]{:S(2)}) collective-permute-start(bf16[8,128,512]{2,1,0:T(8,128)(2,1)} %get-tuple-element.11), channel_id=1, source_target_pairs={{0,2},{1,3},{2,0},{3,1},{4,6},{5,7},{6,4},{7,5},{8,10},{9,11},{10,... | collective-permute-start | bytes 3145736 | tf_op jit(solution)/shard_map/ppermute | solution.py:31
  61.8 13.7 %collective-permute-start.2 = (bf16[2,16,32,128]{3,2,1,0:T(8,128)(2,1)S(1)}, bf16[2,16,32,128]{3,2,1,0:T(8,128)(2,1)S(1)}, u32[]{:S(2)}, u32[]{:S(2)}) collective-permute-start(bf16[2,16,32,128]{3,2,1,0:T(8,128)(2,1)S(1)} %pad_maximum_fusion.1), channel_id=1, source_target_pairs={{0,256},{1,257},{2,258},{3,259},{4,260},{5,261},{6,262},{7,263},{8... | collective-permute-start | bytes 786440 | tf_op jit(solution)/shard_map/ppermute | solution.py:31
  75.6 21.5 %collective-permute-start.3 = (bf16[4,16,32,128]{3,2,1,0:T(8,128)(2,1)S(1)}, bf16[4,16,32,128]{3,2,1,0:T(8,128)(2,1)S(1)}, u32[]{:S(2)}, u32[]{:S(2)}) collective-permute-start(bf16[4,16,32,128]{3,2,1,0:T(8,128)(2,1)S(1)} %pad_maximum_fusion.near_ref), channel_id=1, source_target_pairs={{0,128},{1,129},{2,130},{3,131},{4,132},{5,133},{6,134},{7,135},{8... | collective-permute-start | bytes 1572872 | tf_op jit(solution)/shard_map/ppermute | solution.py:31
  78.7 22.3 %collective-permute-start.5 = (bf16[4,16,32,128]{3,2,1,0:T(8,128)(2,1)S(1)}, bf16[4,16,32,128]{3,2,1,0:T(8,128)(2,1)}, u32[]{:S(2)}, u32[]{:S(2)}) collective-permute-start(bf16[4,16,32,128]{3,2,1,0:T(8,128)(2,1)S(1)} %pad_maximum_fusion.near_ref), channel_id=1, source_target_pairs={{0,16},{1,17},{2,18},{3,19},{4,20},{5,21},{6,22},{7,23},{8,24},{9,... | collective-permute-start | bytes 1572872 | tf_op jit(solution)/shard_map/ppermute | solution.py:31
  84.3 12.7 %collective-permute-start.7 = (f32[32,128]{1,0:T(8,128)S(1)}, f32[32,128]{1,0:T(8,128)S(1)}, u32[]{:S(2)}, u32[]{:S(2)}) collective-permute-start(f32[32,128]{1,0:T(8,128)S(1)} %get-tuple-element.37), channel_id=1, source_target_pairs={{0,16},{1,17},{2,18},{3,19},{4,20},{5,21},{6,22},{7,23},{8,24},{9,... | collective-permute-start | bytes 49160 | tf_op jit(solution)/shard_map/ppermute | solution.py:31
  87.3 1.2 copy-start.1
  91.0 39.2 %all-to-all-start.1 = ((bf16[8,128,512]{2,1,0:T(8,128)(2,1)}), bf16[8,128,512]{2,1,0:T(8,128)(2,1)}, u32[]{:S(2)}, u32[]{:S(2)}) async-start(bf16[8,128,512]{2,1,0:T(8,128)(2,1)} %shard_map.140), calls=%async_computation.1 | async-start | bytes 2097152 | tf_op jit(solution)/shard_map/all_to_all | solution.py:196
  97.1 6.0 %collective-permute-start.4 = (bf16[4,16,32,128]{3,2,1,0:T(8,128)(2,1)S(1)}, bf16[4,16,32,128]{3,2,1,0:T(8,128)(2,1)S(1)}, u32[]{:S(2)}, u32[]{:S(2)}) collective-permute-start(bf16[4,16,32,128]{3,2,1,0:T(8,128)(2,1)S(1)} %collective-permute-done.3.far_ref), channel_id=1, source_target_pairs={{0,16},{1,17},{2,18},{3,19},{4,20},{5,21},{6,22},{7,23},{8,24},{9,... | collective-permute-start | bytes 1572872 | tf_op jit(solution)/shard_map/ppermute | solution.py:31
